TPU v7x, 256 devices: a whole 4x4x8 slice. The times are simulated.
256 devices in a mesh: tm: 8 (over z_lo, core), chan: 32 (over z_hi, y, x).
Axes of the slice: x: 4, y: 4, z: 8 (z_hi: 2, z_lo: 4; z = z_hi * 4 + z_lo), core: 2. Of those that a mesh axis runs over, the one named last changes fastest.
Arguments:
- raw_strain: bfloat16 [256000, 4096], P('tm', 'chan'), may hold values from -600 to 600
- source_blocks: int32 [2], replicated, may hold values from 0 to 27, as said below
- band_bins: int32 [2], replicated, may hold values from 0 to 20, as said below
Outputs:
- cross_spectra: bfloat16 [1280, 2, 20, 4096], P('tm', None, None, 'chan')
Inputs may be any that keep to these rules, and one draw needn't show every extreme that they name: `source_blocks`: each entry is the index of the channel block of 128 channels at which a virtual-source block of 640 channels begins; the two entries differ, one of them is always the last possible start, and the blocks may intersect. band_bins[0] is at most 2 and band_bins[1] is at least 18.
All inputs are finite; a program needn't handle non-finite values.
Results may differ from a plain program's by a relative error of at most 0.0091.
Values may be sent and summed in bfloat16 or wider, within the bound.
A program may use at most 64 MiB of HBM per device.

v0:
```python
import math

import jax
import jax.numpy as jnp
import numpy as np
from jax import lax
from jax.sharding import PartitionSpec as P

NW = 16
WIN = 500
NB = 20
VS = 640
TAPS = 64
DECIM = 4


def from_behind(value, axis, steps):
    count = lax.axis_size(axis)
    initial, last = (max(0, -steps), min(count, count - steps))
    return lax.ppermute(value, axis, [(source, source + steps) for source in range(initial, last)])


def carried_in(part, axis, combine, identity):
    place = lax.axis_index(axis)
    gathered = jax.tree.map(lambda a: lax.all_gather(a, axis), part)
    state = jax.tree.map(lambda a, e: jnp.zeros_like(a) + jnp.asarray(e, a.dtype), part, identity)

    def one(step, state):
        return combine(
            state, jax.tree.map(lambda a: lax.dynamic_index_in_dim(a, step, 0, False), gathered)
        )

    return lax.fori_loop(0, place, one, state)


def lowpass_taps():
    offsets = np.arange(TAPS) - (TAPS - 1) / 2.0
    window = 0.54 - 0.46 * np.cos(2.0 * np.pi * np.arange(TAPS) / (TAPS - 1))
    angles = np.pi * 0.8 * offsets / DECIM
    values = np.sin(angles) / angles * window
    return values / values.sum()


def filter_tables():
    tap_values = lowpass_taps()
    carried = TAPS - DECIM
    outputs = np.arange(WIN)[:, None]
    inputs = np.arange(DECIM * WIN)[None, :]
    lag_main = DECIM * outputs + DECIM - 1 - inputs
    main_table = np.where(
        (lag_main >= 0) & (lag_main < TAPS), tap_values[np.clip(lag_main, 0, TAPS - 1)], 0.0
    )
    earlier_ids = np.arange(carried)[None, :]
    lag_edge = DECIM * outputs + DECIM - 1 - (earlier_ids - carried)
    edge_table = np.where(
        (lag_edge >= 0) & (lag_edge < TAPS), tap_values[np.clip(lag_edge, 0, TAPS - 1)], 0.0
    )
    return (jnp.asarray(main_table, jnp.bfloat16), jnp.asarray(edge_table, jnp.bfloat16))


def running_tables():
    forget = math.exp(-1.0 / WIN)
    step_ids = np.arange(WIN)
    step_gaps = step_ids[:, None] - step_ids[None, :]
    within = np.where(step_gaps >= 0, (1.0 - forget) * forget ** np.maximum(step_gaps, 0), 0.0)
    window_ids = np.arange(NW)
    lag_table = np.arange(NW + 1)[:, None] - 1 - window_ids[None, :]
    carry_table = np.where(lag_table >= 0, forget ** (WIN * np.maximum(lag_table, 0)), 0.0)
    window_powers = forget ** (WIN * window_ids)
    rising = forget ** (step_ids + 1.0)
    return (
        jnp.asarray(within, jnp.float32),
        jnp.asarray(carry_table, jnp.float32),
        jnp.asarray(window_powers, jnp.float32),
        jnp.asarray(rising, jnp.float32),
    )


def spectrum_table():
    time_ids = np.arange(WIN)
    freq_ids = np.arange(1, NB + 1)
    phases = 2.0 * np.pi * freq_ids[:, None] * time_ids[None, :] / WIN
    return jnp.asarray(
        np.concatenate([np.cos(phases), -np.sin(phases)], axis=0) / np.sqrt(WIN), jnp.bfloat16
    )


def gather_groups(whitened):
    return lax.all_gather(whitened[None], "tm", axis=0, tiled=True)


def body(raw_strain, source_blocks, band_bins):
    channels_here = raw_strain.shape[1]
    carried = TAPS - DECIM
    raw_window = DECIM * WIN
    windows = raw_strain.reshape(NW, raw_window, channels_here)
    main_table, edge_table = filter_tables()
    previous = from_behind(raw_strain[NW * raw_window - carried :], "tm", 1)
    earlier = jnp.concatenate([previous[None], windows[: NW - 1, raw_window - carried :]], axis=0)
    decimated = jnp.einsum("mr,wrc->wmc", main_table, windows, preferred_element_type=jnp.float32)
    decimated = decimated + jnp.einsum(
        "mq,wqc->wmc", edge_table, earlier, preferred_element_type=jnp.float32
    )
    within, carry_table, window_powers, rising = running_tables()
    energy = decimated * decimated
    local_run = jnp.einsum("tu,wuc->wtc", within, energy, precision=lax.Precision.HIGHEST)
    window_ends = local_run[:, WIN - 1, :]
    entering = jnp.dot(carry_table, window_ends, precision=lax.Precision.HIGHEST)
    block_total = entering[NW]

    def compose(earlier_map, later_map):
        return (earlier_map[0] * later_map[0], later_map[0] * earlier_map[1] + later_map[1])

    factors = jnp.full((channels_here,), math.exp(-NW), jnp.float32)
    prefix_maps = carried_in(
        (factors, block_total), "tm", compose, (jnp.ones_like(factors), jnp.zeros_like(block_total))
    )
    incoming = prefix_maps[1]
    starts = entering[:NW] + window_powers[:, None] * incoming[None, :]
    running = local_run + rising[None, :, None] * starts[:, None, :]
    normalized = (decimated / jnp.sqrt(jnp.maximum(running, 0.01))).astype(jnp.bfloat16)
    spectra = jnp.einsum(
        "kt,wtc->wkc", spectrum_table(), normalized, preferred_element_type=jnp.float32
    )
    band_power = jnp.sum(spectra * spectra, axis=1) / NB
    bin_index = jnp.arange(NB)
    band_keep = ((bin_index >= band_bins[0]) & (bin_index < band_bins[1])).astype(jnp.float32)
    band_keep = jnp.concatenate([band_keep, band_keep])
    whitened = (
        spectra * band_keep[None, :, None] / jnp.sqrt(jnp.maximum(band_power, 0.1))[:, None, :]
    ).astype(jnp.bfloat16)
    groups = lax.axis_size("tm")
    src_share = 2 * VS // groups
    own_all = gather_groups(whitened)
    gathered = lax.all_gather(whitened, "chan", axis=2, tiled=True)
    first_block = lax.dynamic_slice_in_dim(gathered, source_blocks[0] * channels_here, VS, 2)
    second_block = lax.dynamic_slice_in_dim(gathered, source_blocks[1] * channels_here, VS, 2)
    picked = jnp.concatenate([first_block, second_block], axis=2)
    shares = lax.all_to_all(picked[None], "tm", split_axis=3, concat_axis=0, tiled=True)
    own_spectra = own_all.reshape(groups, NW, 2, NB, channels_here)
    source_groups = shares.reshape(groups, NW, 2, NB, src_share)
    rotated = jnp.stack([-source_groups[:, :, 1], source_groups[:, :, 0]], axis=2)
    turned = jnp.stack([source_groups, rotated], axis=3)
    stack_scale = 1.0 / math.sqrt(groups * NW)

    def add_group(group_index, stacked_sum):
        own_block = lax.dynamic_index_in_dim(own_spectra, group_index, 0, False)
        src_block = lax.dynamic_index_in_dim(turned, group_index, 0, False)
        group_term = (
            jnp.einsum("wpkc,wpqks->sqkc", own_block, src_block, preferred_element_type=jnp.float32)
            * stack_scale
        )
        return stacked_sum + lax.optimization_barrier(group_term.astype(jnp.bfloat16)).astype(
            jnp.float32
        )

    stacked_sum = lax.fori_loop(
        0, groups, add_group, jnp.zeros((src_share, 2, NB, channels_here), jnp.float32)
    )
    return stacked_sum.astype(jnp.bfloat16)


def solution(mesh):
    in_specs = (P("tm", "chan"), P(), P())
    out_specs = P("tm", None, None, "chan")
    return jax.shard_map(body, mesh=mesh, in_specs=in_specs, out_specs=out_specs, check_vma=False)
```

profile of v0, /device:TPU:1, one launch (start us, length us, event | category | flops | bytes accessed | tf_op | source)
XLA Modules:
  0.0 365.0 jit_solution(10536839834026932320)
XLA Ops:
  8.1 4.9 %collective-permute-start = (bf16[60,128]{1,0:T(8,128)(2,1)S(1)}, bf16[60,128]{1,0:T(8,128)(2,1)S(1)}, u32[]{:S(2)}, u32[]{:S(2)}) collective-permute-start(bf16[60,128]{1,0:T(8,128)(2,1)S(1)} %slice.33), channel_id=1, source_target_pairs={{0,32},{32,64},{64,96},{96,128},{128,160},{160,192},{192,224},{1,3... | collective-permute-start | bytes 46088 | tf_op jit(solution)/shard_map/ppermute | solution.py:20
  14.4 10.4 %fusion.15 = f32[500,16,128]{2,0,1:T(8,128)} fusion(bf16[500,2000,1]{0,1,2:T(8,128)(2,1)} %constant.102, bf16[16,2000,128]{2,1,0:T(8,128)(2,1)} %bitcast.88), kind=kOutput, calls=%fused_computation.37 | convolution fusion | flops 4096000000 | bytes 14288000 | tf_op jit(solution)/shard_map/mr,wrc->wmc/dot_general | solution.py:100
  27.2 3.0 bitcast_add_fusion.1
  30.3 7.4 %fusion.4 = f32[16,500,128]{2,1,0:T(8,128)S(1)} fusion(f32[500,500,1]{1,0,2:T(8,128)S(1)} %copy-done.2, f32[16,128,500]{1,2,0:T(8,128)S(1)} %bitcast_add_fusion.1), kind=kOutput, calls=%fused_computation.16 | convolution fusion | flops 6145024000 | bytes 9192000 | tf_op jit(solution)/shard_map/tu,wuc->wtc/dot_general | solution.py:106
  39.8 11.2 %all-gather.1 = f32[8,1,128]{2,1,0:T(1,128)S(1)} all-gather(f32[1,1,128]{2,1,0:T(1,128)S(1)} %slice_bitcast_fusion), channel_id=1, replica_groups=mesh['tm'=8,'chan'=32] {'tm'}, dimensions={0}, use_global_device_ids=true | all-gather | bytes 4608 | tf_op jit(solution)/shard_map/all_gather | solution.py:25
  51.4 4.4 %multiply_reduce_fusion = (f32[16,128]{1,0:T(8,128)S(1)}, f32[16,128,40]{1,2,0:T(8,128)S(1)}) fusion(bf16[40,500,1]{1,0,2:T(8,128)(2,1)S(1)} %copy-done.4, f32[16,128,500]{1,2,0:T(8,128)} %copy-done, f32[16,500,128]{2,1,0:T(8,128)} %copy-done.1, f32[16,128]{1,0:T(8,128)S(1)} %slice_add_fusion, f32[500]{0:T(512)S(1)} %copy-done.7), kind=kOutput, calls=%fused_computation.21 | convolution fusion | flops 87201792 | bytes 8578064 | tf_op jit(solution)/shard_map/kt,wtc->wkc/dot_general | solution.py:122
  58.5 149.2 %all-gather.5.cloned.1.call-done = bf16[16,40,4096]{2,1,0:T(8,128)(2,1)} async-done(((bf16[16,40,128]{2,1,0:T(8,128)(2,1)}), bf16[16,40,4096]{2,1,0:T(8,128)(2,1)}) %all-gather.5.cloned.1.call-update) | async-done | bytes 5242896 | tf_op jit(solution)/shard_map/all_gather | solution.py:135
  209.4 5.7 %copy.23 = bf16[1,16,40,1280]{2,1,0,3:T(8,128)(2,1)} copy(bf16[1,16,40,1280]{3,2,1,0:T(8,128)(2,1)S(1)} %maximum_bitcast_fusion.1) | data formatting | bytes 3276800 | tf_op jit(solution)/shard_map/broadcast_in_dim | solution.py:139
  215.1 10.2 %reshape.38 = bf16[8,2,51200]{2,1,0:T(2,128)(2,1)} reshape(bf16[1280,1,16,40]{3,2,1,0:T(8,128)(2,1)} %bitcast.81) | data formatting | bytes 3276800
  225.3 5.8 %all-to-all-start = ((bf16[8,2,51200]{2,1,0:T(2,128)(2,1)}), bf16[8,2,51200]{2,1,0:T(2,128)(2,1)}, u32[]{:S(2)}, u32[]{:S(2)}) async-start(bf16[8,2,51200]{2,1,0:T(2,128)(2,1)} %reshape.38), calls=%async_computation | async-start | bytes 3276800 | tf_op jit(solution)/shard_map/all_to_all | solution.py:139
  231.6 50.4 %all-gather.7.cloned.1.call-done = bf16[128,40,128]{2,1,0:T(8,128)(2,1)} async-done(((bf16[16,40,128]{2,1,0:T(8,128)(2,1)}), bf16[128,40,128]{2,1,0:T(8,128)(2,1)}) %all-gather.7.cloned.1.call-update) | async-done | bytes 1310736 | tf_op jit(solution)/shard_map/all_gather | solution.py:89
  284.8 10.4 %reshape.39 = bf16[1280,1,16,40]{3,2,1,0:T(8,128)(2,1)} reshape(bf16[8,2,51200]{2,1,0:T(2,128)(2,1)} %all-to-all-done) | data formatting | bytes 3276800
  295.2 8.5 %copy.33 = bf16[1,16,40,8,160]{4,3,2,1,0:T(8,128)(2,1)} copy(bf16[1,16,40,8,160]{2,1,4,3,0:T(8,128)(2,1)} %bitcast.82) | data formatting | bytes 3276800 | tf_op jit(solution)/shard_map/all_to_all | solution.py:139
  303.7 3.2 copy.25
  307.6 3.3 pad_maximum_fusion
  310.9 43.9 %while.28 = (s32[]{:T(128)}, f32[160,2,20,128]{3,0,1,2:T(8,128)S(1)}, bf16[8,16,2,2,20,160]{5,1,4,2,0,3:T(8,128)(2,1)}, bf16[8,16,2,20,128]{4,1,0,3,2:T(8,128)(2,1)}, s32[]{:T(128)}, /*index=5*/s32[]{:T(128)}) while((s32[]{:T(128)}, f32[160,2,20,128]{3,0,1,2:T(8,128)S(1)}, bf16[8,16,2,2,20,160]{5,1,4,2,0,3:T(8,128)(2,1)}, ...), condition=%wide.region_4.5_spmd.clone, body=%wide.region_3.4_spmd.clone.sunk | while | flops 56524800 | bytes 10650703 | solution.py:157
  310.9 3.0 fusion.25
  316.4 3.0 fusion.25
  321.9 3.0 fusion.25
  327.4 3.0 fusion.25
  332.9 3.0 fusion.25
  338.4 3.0 fusion.25
  343.9 3.0 fusion.25
  349.4 3.0 fusion.25
  (55 shorter events, 36.5 us)
Async XLA Ops:
  7.4 200.3 %all-gather.5.cloned.1.call-start = ((), (), s32[]{:S(2)}) async-start(), calls=%async_computation.1 | async-start | bytes 5406720 | tf_op jit(solution)/shard_map/all_gather | solution.py:135
  8.1 19.1 %collective-permute-start = (bf16[60,128]{1,0:T(8,128)(2,1)S(1)}, bf16[60,128]{1,0:T(8,128)(2,1)S(1)}, u32[]{:S(2)}, u32[]{:S(2)}) collective-permute-start(bf16[60,128]{1,0:T(8,128)(2,1)S(1)} %slice.33), channel_id=1, source_target_pairs={{0,32},{32,64},{64,96},{96,128},{128,160},{160,192},{192,224},{1,3... | collective-permute-start | bytes 46088 | tf_op jit(solution)/shard_map/ppermute | solution.py:20
  14.4 12.8 %copy-start.3 = (bf16[500,60,1]{0,1,2:T(8,128)(2,1)S(1)}, bf16[500,60,1]{0,1,2:T(8,128)(2,1)}, u32[]{:S(2)}) copy-start(bf16[500,60,1]{0,1,2:T(8,128)(2,1)} %constant.103) | copy-start | bytes 180004
  27.2 3.0 copy-start.2
  30.2 7.5 %copy-start = (f32[16,128,500]{1,2,0:T(8,128)}, f32[16,128,500]{1,2,0:T(8,128)S(1)}, u32[]{:S(2)}) copy-start(f32[16,128,500]{1,2,0:T(8,128)S(1)} %bitcast_add_fusion.1) | copy-start | bytes 12288004
  30.2 9.4 %copy-start.5 = (f32[17,16]{1,0:T(8,128)S(1)}, f32[17,16]{1,0:T(8,128)}, u32[]{:S(2)}) copy-start(f32[17,16]{1,0:T(8,128)} %constant.98.clone) | copy-start | bytes 3268
  30.2 21.0 %copy-start.8 = (f32[16]{0:T(128)S(1)}, f32[16]{0:T(128)}, u32[]{:S(2)}) copy-start(f32[16]{0:T(128)} %constant.99.clone) | copy-start | bytes 196
  30.2 21.1 %copy-start.4 = (bf16[40,500,1]{1,0,2:T(8,128)(2,1)S(1)}, bf16[40,500,1]{1,0,2:T(8,128)(2,1)}, u32[]{:S(2)}) copy-start(bf16[40,500,1]{1,0,2:T(8,128)(2,1)} %constant.105) | copy-start | bytes 120004
  30.3 21.1 %copy-start.7 = (f32[500]{0:T(512)S(1)}, f32[500]{0:T(512)}, u32[]{:S(2)}) copy-start(f32[500]{0:T(512)} %constant.100.clone) | copy-start | bytes 6004
  37.7 2.0 copy-start.1
  51.4 5.3 %copy-start.6 = (s32[2]{0:T(128)S(1)}, s32[2]{0:T(128)}, u32[]{:S(2)}) copy-start(s32[2]{0:T(128)} %param.15) | copy-start | bytes 28
  225.3 59.5 %all-to-all-start = ((bf16[8,2,51200]{2,1,0:T(2,128)(2,1)}), bf16[8,2,51200]{2,1,0:T(2,128)(2,1)}, u32[]{:S(2)}, u32[]{:S(2)}) async-start(bf16[8,2,51200]{2,1,0:T(2,128)(2,1)} %reshape.38), calls=%async_computation | async-start | bytes 3276800 | tf_op jit(solution)/shard_map/all_to_all | solution.py:139
  231.1 51.0 %all-gather.7.cloned.1.call-start = ((), (), s32[]{:S(2)}) async-start(), calls=%async_computation.2 | async-start | bytes 1474560 | tf_op jit(solution)/shard_map/all_gather | solution.py:89
Sparse Core Ops, SparseCore 0:
  56.7 150.9 all-gather.4
Sparse Core Ops, SparseCore 1:
  233.3 48.7 all-gather.6
where the time goes:
time: 366 us; the launch traced here: 365 us
  waiting for transfers between devices  200 us (55%)
  local copies, waits for them, and re-layouts  50.5 us (14%)
  matrix products  49.2 us (13%)
  other arithmetic  26.5 us (7%)
  between operations  16.4 us (4%)
  blocking collectives  11.2 us (3%)
  starting transfers between devices  10.7 us (3%)
    all_gather x1, waiting for transfers between devices, body(): gathered = lax.all_gather(whitened, 'chan', axis=2, tiled=True)  149 us
    all_gather x1, waiting for transfers between devices, gather_groups(): return lax.all_gather(whitened[None], 'tm', axis=0, tiled=True)  50.4 us
    dot_general x8, matrix products, add_group(): jnp.einsum('wpkc,wpqks->sqkc', own_block, src_block, preferred_element_ty...  23.8 us
    unnamed x21, local copies, waits for them, and re-layouts  22.6 us
    add x8, other arithmetic, add_group(): stacked_sum + lax.optimization_barrier(group_term.astype(jnp.bfloat16)).a...  20 us
    all_to_all x2, local copies, waits for them, and re-layouts, body(): lax.all_to_all(picked[None], 'tm', split_axis=3, concat_axis=0, tiled=True)  11.7 us
    all_gather x1, blocking collectives, carried_in(): gathered = jax.tree.map(lambda a: lax.all_gather(a, axis), part)  11.2 us
    dot_general x1, matrix products, body(): jnp.einsum('mr,wrc->wmc', main_table, windows, preferred_element_type=jnp...  10.4 us
  transfers between devices with their start and end apart: 4, of which 2 were waited for; matrix products, arithmetic and copies ran while one was open for 5% of the time, Pallas kernels for 0%

commit v1 on v0

v1 whole, which is shorter than its diff:
```python
import functools
import math

import jax
import jax.numpy as jnp
import numpy as np
from jax import lax
from jax.experimental import pallas as pl
from jax.experimental.pallas import tpu as pltpu
from jax.sharding import PartitionSpec as P

NW = 16
WIN = 500
NB = 20
VS = 640
TAPS = 64
DECIM = 4
CH = 128
ROWS = DECIM * NW * WIN
OUTS = NW * WIN
MB = 112
KB = 512
STEP = DECIM * MB
PAIRS = 36
HALO = 64
RAW_PAD = HALO + 2 * PAIRS * STEP
DEC_PAD = 2 * PAIRS * MB
EB = 256
EN_PAD = 8192
CHUNKS = 5
CROWS = ROWS // CHUNKS
MAIN = 16
AR = 40
SR = 56
QR = 400
SHARE = 160
PARTS = ((0, 112), (112, 96), (208, 96), (304, 96))
FORGET = math.exp(-1.0 / WIN)
F32 = jnp.float32
BF16 = jnp.bfloat16
MESH = pl.DeviceIdType.MESH


def lowpass_taps():
    offsets = np.arange(TAPS) - (TAPS - 1) / 2.0
    window = 0.54 - 0.46 * np.cos(2.0 * np.pi * np.arange(TAPS) / (TAPS - 1))
    angles = np.pi * 0.8 * offsets / DECIM
    values = np.sin(angles) / angles * window
    return values / values.sum()


def tables():
    taps = lowpass_taps()
    lag = DECIM * np.arange(MB)[:, None] + DECIM - 1 + HALO - np.arange(KB)[None, :]
    decim = np.where((lag >= 0) & (lag < TAPS), taps[np.clip(lag, 0, TAPS - 1)], 0.0)
    gap = np.arange(EB)[:, None] - np.arange(EB)[None, :]
    within = np.where(gap >= 0, (1.0 - FORGET) * FORGET ** np.maximum(gap, 0), 0.0)
    rising = np.broadcast_to((FORGET ** (np.arange(EB) + 1.0))[:, None], (EB, CH))
    tail = OUTS - (2 * PAIRS - 1) * MB
    rows = np.arange(MB)
    full = (1.0 - FORGET) * FORGET ** (MB - 1.0 - rows)
    last = np.where(rows < tail, (1.0 - FORGET) * FORGET ** np.maximum(tail - 1.0 - rows, 0.0), 0.0)
    weights = np.broadcast_to(np.stack([full, last])[:, :, None], (2, MB, CH))
    phases = 2.0 * np.pi * np.arange(1, NB + 1)[:, None] * np.arange(WIN)[None, :] / WIN
    cos, sin = np.cos(phases) / np.sqrt(WIN), -np.sin(phases) / np.sqrt(WIN)
    ordered = np.concatenate([cos[:MAIN], sin[:MAIN], cos[MAIN:], sin[MAIN:]], axis=0)
    dft = np.zeros((4, 2 * NB, 512))
    for place in range(4):
        dft[place, :, 4 * place : 4 * place + WIN] = ordered
    return (
        jnp.asarray(decim, BF16),
        jnp.asarray(within, BF16),
        jnp.asarray(dft, BF16),
        jnp.asarray(rising, F32),
        jnp.asarray(weights, F32),
    )


def kernel(
    blocks_ref, band_ref, raw_ref, decim_ref, within_ref, dft_ref, rising_ref, weights_ref, out_ref,
    raw_v, dec_v, en_v, run_v, norm_v, white_v, total_v, totals_v, own_v, first_v, share_v, shares_v,
    pieces_v, acc_v,
    raw_sem, halo_sem, tot_ssem, tot_rsem, a_ssem, a_rsem, b_ssem, b_rsem, own_ssem, own_rsem,
    q_ssem, q_rsem,
):
    tm = lax.axis_index("tm")
    chan = lax.axis_index("chan")
    zl, core = tm // 2, tm % 2
    zh, pid = chan // 16, chan % 16
    y, x = pid // 4, pid % 4
    line = zh * 8 + tm

    def plane_peer(step):
        other = (pid + step) % 16
        return other, (tm, zh * 16 + other)

    def line_peer(step):
        other = (line + step) % 16
        return other, (other % 8, (other // 8) * 16 + pid)

    totals_v[...] = jnp.zeros(totals_v.shape, F32)

    barrier = pltpu.get_barrier_semaphore()
    for step in range(1, 16):
        pl.semaphore_signal(barrier, inc=1, device_id=plane_peer(step)[1], device_id_type=MESH)
        pl.semaphore_signal(barrier, inc=1, device_id=line_peer(step)[1], device_id_type=MESH)

    def chunk(c):
        return pltpu.make_async_copy(
            raw_ref.at[pl.ds(c * CROWS, CROWS)],
            raw_v.at[pl.ds(HALO + c * CROWS, CROWS)],
            raw_sem.at[c],
        )

    for c in range(CHUNKS):
        chunk(c).start()
    raw_v[HALO + ROWS : RAW_PAD, :] = jnp.zeros((RAW_PAD - HALO - ROWS, CH), BF16)
    en_v[DEC_PAD:EN_PAD, :] = jnp.zeros((EN_PAD - DEC_PAD, CH), BF16)
    dec_v[DEC_PAD:EN_PAD, :] = jnp.zeros((EN_PAD - DEC_PAD, CH), F32)

    @pl.when(tm == 0)
    def _():
        raw_v[0:HALO, :] = jnp.zeros((HALO, CH), BF16)

    def halo_to(other):
        return pltpu.make_async_remote_copy(
            src_ref=raw_ref.at[pl.ds(ROWS - HALO, HALO)],
            dst_ref=raw_v.at[pl.ds(0, HALO)],
            send_sem=halo_sem.at[0],
            recv_sem=halo_sem.at[1],
            device_id=(other, chan),
            device_id_type=MESH,
        )

    block_fade = FORGET**MB
    tail = OUTS - (2 * PAIRS - 1) * MB

    def decimate(pair, last):
        start = pl.multiple_of(pair * (2 * STEP), 128)
        left = raw_v[pl.ds(start, KB), :]
        right = raw_v[pl.ds(start + STEP, KB), :]
        both = jnp.dot(
            decim_ref[...], jnp.concatenate([left, right], axis=1), preferred_element_type=F32
        )
        row = pl.multiple_of(pair * (2 * MB), 32)
        sums = []
        for half in range(2):
            values = both[:, half * CH : (half + 1) * CH]
            dec_v[pl.ds(row + half * MB, MB), :] = values
            energy = values * values
            en_v[pl.ds(row + half * MB, MB), :] = energy.astype(BF16)
            weights = weights_ref[1 if (last and half == 1) else 0]
            sums.append(jnp.sum((weights * energy).reshape(MB // 8, 8, CH), axis=0))
        return sums[0] * (FORGET**tail if last else block_fade) + sums[1]

    def advance(pair, total):
        return total * (block_fade * block_fade) + decimate(pair, False)

    total = jnp.zeros((8, CH), F32)
    for c in range(CHUNKS):
        chunk(c).wait()
        if c == 2:
            pl.semaphore_wait(barrier, 30)

            @pl.when(tm < 7)
            def _():
                halo_to(tm + 1).start()

        total = lax.fori_loop(max(1, 7 * c), 7 * c + 7, advance, total)
    total = total * (block_fade * FORGET**tail) + decimate(PAIRS - 1, True)

    @pl.when(tm > 0)
    def _():
        halo_to(tm - 1).wait_recv()

    total = total + decimate(0, False) * FORGET ** (OUTS - 2 * MB)
    total_v[...] = jnp.broadcast_to(jnp.sum(total, axis=0, keepdims=True), (8, CH))

    def total_to(other, place, step):
        return pltpu.make_async_remote_copy(
            src_ref=total_v,
            dst_ref=totals_v.at[place],
            send_sem=tot_ssem.at[step],
            recv_sem=tot_rsem.at[place],
            device_id=(other, chan),
            device_id_type=MESH,
        )

    for step in range(1, 8):

        @pl.when(tm + step < 8)
        def _():
            total_to(tm + step, tm, step).start()

    def local_run(pair, carry):
        row = pl.multiple_of(pair * (2 * EB), 2 * EB)
        rhs = jnp.concatenate([en_v[pl.ds(row, EB), :], en_v[pl.ds(row + EB, EB), :]], axis=1)
        both = jnp.dot(within_ref[...], rhs, preferred_element_type=F32)
        run_v[pl.ds(row, EB), :] = both[:, :CH]
        run_v[pl.ds(row + EB, EB), :] = both[:, CH:]
        return carry

    lax.fori_loop(0, EN_PAD // (2 * EB), local_run, 0)

    for place in range(7):

        @pl.when(place < tm)
        def _():
            total_to(tm, place, 0).wait_recv()

    state = jnp.zeros((8, CH), F32)
    for place in range(7):
        state = jnp.where(place < tm, state * math.exp(-NW) + totals_v[place], state)

    def normalize(block, state):
        row = pl.multiple_of(block * EB, EB)
        running = run_v[pl.ds(row, EB), :] + rising_ref[...] * state[0:1, :]
        values = dec_v[pl.ds(row, EB), :] * lax.rsqrt(jnp.maximum(running, 0.01))
        norm_v[pl.ds(row, EB), :] = values.astype(BF16)
        return jnp.broadcast_to(running[EB - 1 : EB, :], (8, CH))

    lax.fori_loop(0, OUTS // EB + 1, normalize, state)

    low, high = band_ref[0], band_ref[1]
    row_id = lax.broadcasted_iota(jnp.int32, (2 * NB, CH), 0)
    bin_id = jnp.where(row_id < 2 * MAIN, row_id % MAIN, MAIN + row_id % 4)
    keep = jnp.where((bin_id >= low) & (bin_id < high), 1.0, 0.0).astype(F32)
    for first in range(NW):
        if first % 8 >= 4:
            continue
        start = (first * WIN) // 16 * 16
        rhs = jnp.concatenate(
            [norm_v[pl.ds(start, 512), :], norm_v[pl.ds(start + 4 * WIN, 512), :]], axis=1
        )
        both = jnp.dot(dft_ref[(first * WIN) % 16 // 4], rhs, preferred_element_type=F32)
        for half in range(2):
            w = first + 4 * half
            spectra = both[:, half * CH : (half + 1) * CH]
            power = jnp.sum(spectra * spectra, axis=0, keepdims=True) / NB
            white = spectra * keep * lax.rsqrt(jnp.maximum(power, 0.1))
            for p in range(2):
                white_v[pl.ds(p * NW + w, MAIN, stride=AR), :] = white[p * MAIN : (p + 1) * MAIN]
                white_v[pl.ds(w // 4 * (4 * AR) + 32 + p * 4 + w % 4, 4, stride=AR), :] = white[
                    32 + 4 * p : 36 + 4 * p
                ]
    own_v[tm] = white_v[...].reshape(MAIN, AR, CH).astype(BF16)

    def plane_copy(other, device, step, place):
        return pltpu.make_async_remote_copy(
            src_ref=own_v.at[tm, other],
            dst_ref=first_v.at[place],
            send_sem=a_ssem.at[step],
            recv_sem=a_rsem.at[place],
            device_id=device,
            device_id_type=MESH,
        )

    for step in range(1, 16):
        other, device = plane_peer(step)
        plane_copy(other, device, step, pid).start()

    def own_copy(group, other, slot):
        return pltpu.make_async_remote_copy(
            src_ref=own_v.at[group],
            dst_ref=own_v.at[group],
            send_sem=own_ssem.at[slot],
            recv_sem=own_rsem.at[group],
            device_id=(other, chan),
            device_id_type=MESH,
        )

    partner = zl * 2 + 1 - core
    sends = [(None, tm, partner, 0), (zl < 3, tm, tm + 2, 1), (zl > 0, tm, tm - 2, 2)]

    def start_send(entry):
        condition, group, other, slot = entry
        if condition is None:
            own_copy(group, other, slot).start()
        else:

            @pl.when(condition)
            def _():
                own_copy(group, other, slot).start()

    for entry in sends:
        start_send(entry)

    first_v[pid] = own_v[tm, pid]
    for step in range(1, 16):
        other, device = plane_peer(step)
        plane_copy(pid, device, 0, other).wait_recv()

    lane8 = lax.broadcasted_iota(jnp.int32, (8, CH), 1)
    lane40 = lax.broadcasted_iota(jnp.int32, (AR, CH), 1)
    for b in range(2):
        picked = []
        for i in range(5):
            block = blocks_ref[b] + i
            here = jnp.where(block // 16 == zh, 1.0, 0.0).astype(F32)
            picked.append(first_v[block % 16].astype(F32) * here)
        for jj in range(4):
            a, c = picked[jj], picked[jj + 1]
            if jj == 0:
                head = a
            else:
                turn = CH - 32 * jj
                head = jnp.where(
                    lane40 < turn, pltpu.roll(a, turn, axis=1), pltpu.roll(c, turn, axis=1)
                )
            rest = jnp.zeros((8, CH), F32)
            for q in range(5):
                turn = (32 * (q % 4) - 32 * jj) % CH
                part = c[8 * q : 8 * q + 8]
                part = pltpu.roll(part, turn, axis=1) if turn else part
                low_lane = 32 * (q % 4)
                part = jnp.where((lane8 >= low_lane) & (lane8 < low_lane + 32), part, 0.0)
                if q < 4:
                    rest = rest + part
                else:
                    last_rest = part
            share_v[b * 4 + jj] = jnp.concatenate([head, rest, last_rest], axis=0).astype(BF16)

    def line_copy(share, device, step, place):
        return pltpu.make_async_remote_copy(
            src_ref=share_v.at[share],
            dst_ref=shares_v.at[place],
            send_sem=b_ssem.at[step],
            recv_sem=b_rsem.at[place],
            device_id=device,
            device_id_type=MESH,
        )

    for step in range(1, 16):
        other, device = line_peer(step)
        line_copy(other % 8, device, step, line).start()
    shares_v[line] = share_v[tm]
    for step in range(1, 16):
        other, device = line_peer(step)
        line_copy(tm, device, 0, other).wait_recv()

    mains, tails = [], []
    for g in range(8):
        both = shares_v[g].astype(F32) + shares_v[8 + g].astype(F32)
        rests = []
        for q in range(5):
            packed = both[40:48] if q < 4 else both[48:56]
            turn = (CH - 32 * (q % 4)) % CH
            rests.append(pltpu.roll(packed, turn, axis=1) if turn else packed)
        rows = jnp.concatenate([both[0:40], jnp.concatenate(rests, axis=0)], axis=1)
        mains.append(rows[0:32])
        tails.append(rows[32:40])
    mains = jnp.concatenate(mains, axis=0).astype(BF16)
    tails = jnp.concatenate(tails + tails, axis=0).astype(BF16)
    eye = (
        lax.broadcasted_iota(jnp.int32, (SHARE, 256), 0)
        == lax.broadcasted_iota(jnp.int32, (SHARE, 256), 1)
    )
    eye = jnp.where(eye, 1.0, 0.0).astype(BF16)
    contract = (((1,), (1,)), ((), ()))
    turned = lax.dot_general(eye, mains, contract, preferred_element_type=F32)
    turned_tail = lax.dot_general(eye, tails, contract, preferred_element_type=F32)
    half_lane = lax.broadcasted_iota(jnp.int32, (80, CH), 1) < 64
    packed_tail = jnp.where(half_lane, turned_tail[0:80], turned_tail[80:160])
    pieces_v[pid] = jnp.concatenate([turned[:, :CH], turned[:, CH:], packed_tail], axis=0).astype(
        BF16
    )

    def at(dx, dy):
        return ((y + dy) % 4) * 4 + (x + dx) % 4

    def piece_copy(source, part, direction):
        dx, dy = ((1, 0), (3, 0), (0, 1), (0, 3))[direction]
        first, count = PARTS[part]
        rows = pl.ds(first, count)
        return pltpu.make_async_remote_copy(
            src_ref=pieces_v.at[source, rows],
            dst_ref=pieces_v.at[source, rows],
            send_sem=q_ssem.at[source, part, direction],
            recv_sem=q_rsem.at[source, part],
            device_id=(tm, zh * 16 + at(dx, dy)),
            device_id_type=MESH,
        )

    piece_sends = []

    def piece_send(source, part, direction):
        piece_copy(source, part, direction).start()
        piece_sends.append((source, part, direction))

    def piece_wait(source, part):
        piece_copy(source, part, 0).wait_recv()

    for part in range(4):
        axis = 0 if part < 2 else 2
        piece_send(pid, part, axis)
        piece_send(pid, part, axis + 1)
    for part in range(4):
        axis = 2 if part < 2 else 0
        piece_send(pid, part, axis)
        piece_send(pid, part, axis + 1)

    for step in range(1, 4):
        below, above = tm - 2 * step, tm + 2 * step

        @pl.when(zl - step >= 0)
        def _():
            own_copy(below, partner, 0).wait_recv()

        entry = (zl - step >= 0, below, partner, 3 * step)
        start_send(entry)
        sends.append(entry)
        if step < 3:
            entry = ((zl - step >= 0) & (zl < 3), below, tm + 2, 3 * step + 1)
            start_send(entry)
            sends.append(entry)

        @pl.when(zl + step <= 3)
        def _():
            own_copy(above, partner, 0).wait_recv()

        entry = (zl + step <= 3, above, partner, 9 + 3 * step)
        start_send(entry)
        sends.append(entry)
        if step < 3:
            entry = ((zl + step <= 3) & (zl > 0), above, tm - 2, 9 + 3 * step + 1)
            start_send(entry)
            sends.append(entry)
        if step == 1:
            relay_pieces(at, piece_send, piece_wait)
    finish_pieces(at, piece_send, piece_wait)

    for other_zl in range(4):
        own_copy(other_zl * 2 + 1 - core, partner, 0).wait_recv()

    scale = 1.0 / math.sqrt(8 * NW)

    def put(k, lhs, rhs):
        both = jnp.dot(lhs, rhs, preferred_element_type=F32) * scale
        acc_v[pl.ds(k, SHARE, stride=48), :] = both[:, :CH]
        acc_v[pl.ds(24 + k, SHARE, stride=48), :] = both[:, CH:]

    def main_bin(k, carry):
        lhs = jnp.concatenate([pieces_v[k, 0:SHARE], pieces_v[k, SHARE : 2 * SHARE]], axis=1)
        re, im = [], []
        for g in range(8):
            rows = own_v[g, k, 0:32]
            re.append(rows)
            im.append(rows[16:32])
            im.append(-rows[0:16])
        rhs = jnp.concatenate([jnp.concatenate(re, axis=0), jnp.concatenate(im, axis=0)], axis=1)
        put(k, lhs, rhs)
        return carry

    lax.fori_loop(0, MAIN, main_bin, 0)

    sign = jnp.where(lax.broadcasted_iota(jnp.int32, (8, CH), 0) < 4, 1.0, -1.0).astype(F32)

    def tail_bin(kk, carry):
        columns = []
        for pair in range(2):
            even = pieces_v[pair * 8 + kk, 2 * SHARE : QR].astype(F32)
            odd = pieces_v[pair * 8 + 4 + kk, 2 * SHARE : QR].astype(F32)
            upper = jnp.where(half_lane, even, pltpu.roll(odd, 64, axis=1))
            lower = jnp.where(half_lane, pltpu.roll(even, 64, axis=1), odd)
            columns.append(jnp.concatenate([upper, lower], axis=0))
        lhs = jnp.concatenate(columns, axis=1).astype(BF16)
        re, im = [], []
        for wh in range(4):
            for g in range(8):
                rows = own_v[g, wh * 4 + kk, 32:40].astype(F32)
                re.append(rows)
                im.append(pltpu.roll(rows, 4, axis=0) * sign)
        rhs = jnp.concatenate([jnp.concatenate(re, axis=0), jnp.concatenate(im, axis=0)], axis=1)
        put(MAIN + kk, lhs, rhs.astype(BF16))
        return carry

    lax.fori_loop(0, NB - MAIN, tail_bin, 0)

    def give(chunk_id, carry):
        row = pl.multiple_of(chunk_id * (8 * 48), 8 * 48)
        values = acc_v[pl.ds(row, 8 * 48), :].reshape(8, 2, 24, CH)
        out_ref[pl.ds(chunk_id * 8, 8)] = values[:, :, :NB, :].astype(BF16)
        return carry

    lax.fori_loop(0, SHARE // 8, give, 0)

    @pl.when(tm < 7)
    def _():
        halo_to(tm + 1).wait_send()

    for step in range(1, 8):

        @pl.when(tm + step < 8)
        def _():
            total_to(tm + step, tm, step).wait_send()

    for step in range(1, 16):
        other, device = plane_peer(step)
        plane_copy(other, device, step, pid).wait_send()
        other, device = line_peer(step)
        line_copy(other % 8, device, step, line).wait_send()
    for condition, group, other, slot in sends:
        if condition is None:
            own_copy(group, other, slot).wait_send()
        else:

            @pl.when(condition)
            def _():
                own_copy(group, other, slot).wait_send()

    for entry in piece_sends:
        piece_copy(*entry).wait_send()


def relay_pieces(at, send, wait):
    for part in range(4):
        along = 0 if part < 2 else 2
        across = 2 - along
        for toward in range(2):
            offset = 3 if toward == 0 else 1
            source = at(offset, 0) if along == 0 else at(0, offset)
            wait(source, part)
            if part % 2 == toward:
                send(source, part, along + toward)
            send(source, part, across)
            send(source, part, across + 1)


def finish_pieces(at, send, wait):
    for part in range(4):
        along = 0 if part < 2 else 2
        across = 2 - along

        def place(first, second):
            return at(first, second) if along == 0 else at(second, first)

        for first in (0, 1, 3, 2):
            if first == 2:
                source = place(2, 0)
                wait(source, part)
                send(source, part, across)
                send(source, part, across + 1)
            for toward in range(2):
                source = place(first, 3 if toward == 0 else 1)
                wait(source, part)
                if part % 2 == toward:
                    send(source, part, across + toward)
    for part in range(4):
        along = 0 if part < 2 else 2
        for first in range(4):
            wait(at(first, 2) if along == 0 else at(2, first), part)


def body(raw_strain, source_blocks, band_bins):
    decim, within, dft, rising, weights = tables()
    smem = pl.BlockSpec(memory_space=pltpu.SMEM)
    vmem = pl.BlockSpec(memory_space=pltpu.VMEM)
    dma = pltpu.SemaphoreType.DMA
    return pl.pallas_call(
        kernel,
        out_shape=jax.ShapeDtypeStruct((SHARE, 2, NB, CH), BF16),
        in_specs=[smem, smem, pl.BlockSpec(memory_space=pl.ANY), vmem, vmem, vmem, vmem, vmem],
        out_specs=vmem,
        scratch_shapes=[
            pltpu.VMEM((RAW_PAD, CH), BF16),
            pltpu.VMEM((EN_PAD, CH), F32),
            pltpu.VMEM((EN_PAD, CH), BF16),
            pltpu.VMEM((EN_PAD, CH), F32),
            pltpu.VMEM((EN_PAD, CH), BF16),
            pltpu.VMEM((MAIN * AR, CH), F32),
            pltpu.VMEM((8, CH), F32),
            pltpu.VMEM((8, 8, CH), F32),
            pltpu.VMEM((8, MAIN, AR, CH), BF16),
            pltpu.VMEM((16, AR, CH), BF16),
            pltpu.VMEM((8, SR, CH), BF16),
            pltpu.VMEM((16, SR, CH), BF16),
            pltpu.VMEM((16, QR, CH), BF16),
            pltpu.VMEM((SHARE * 48, CH), F32),
            dma((CHUNKS,)),
            dma((2,)),
            dma((8,)),
            dma((8,)),
            dma((16,)),
            dma((16,)),
            dma((16,)),
            dma((16,)),
            dma((20,)),
            dma((8,)),
            dma((16, 4, 4)),
            dma((16, 4)),
        ],
        compiler_params=pltpu.CompilerParams(
            collective_id=0, has_side_effects=True, vmem_limit_bytes=60 * 2**20
        ),
        name="cross_spectra",
    )(source_blocks, band_bins, raw_strain, decim, within, dft, rising, weights)


def solution(mesh):
    in_specs = (P("tm", "chan"), P(), P())
    out_specs = P("tm", None, None, "chan")
    return jax.shard_map(body, mesh=mesh, in_specs=in_specs, out_specs=out_specs, check_vma=False)
```

time: 366 us -> 77.9 us (0.21)
  the two profiles are of different devices: /device:TPU:1 before, /device:TPU:4 now
where the time goes in v1:
time: 77.9 us; the launch traced here: 77.7 us
  Pallas kernels  73.4 us (94%)
  local copies, waits for them, and re-layouts  4.31 us (6%)
    pallas_call x1, Pallas kernels, body(): pl.pallas_call(kernel, out_shape=jax.ShapeDtypeStruct((SHARE, 2, NB, CH),...  73.4 us
    pallas_call x1, local copies, waits for them, and re-layouts, body(): pl.pallas_call(kernel, out_shape=jax.ShapeDtypeStruct((SHARE, 2, NB, CH),...  4.31 us

profile of v1, /device:TPU:4, one launch (start us, length us, event | category | flops | bytes accessed | tf_op | source)
XLA Modules:
  0.0 77.7 jit_solution(121717613257278581)
XLA Ops:
  0.0 73.4 %cross_spectra.1 = bf16[160,2,20,128]{3,2,1,0:T(8,128)(2,1)} custom-call(s32[2]{0:T(128)} %blocks_ref.1, s32[2]{0:T(128)} %band_ref.1, bf16[32000,128]{1,0:T(8,128)(2,1)} %raw_ref.1, bf16[112,512]{1,0:T(8,128)(2,1)} %constant.10.clone.decim_ref, bf16[256,256]{1,0:T(8,128)(2,1)} %constant.11.clone.within_ref, bf16[4,40,512]{2,1,0:T(8,128)(2,1)} %constant.12.clone.dft_ref, ...), custom_call_target="tpu_custom_call" | custom-call | tf_op jit(solution)/shard_map/cross_spectra/pallas_call | solution.py:559
  73.4 4.3 %copy.9 = bf16[160,2,20,128]{3,1,2,0:T(2,128)(2,1)} copy(bf16[160,2,20,128]{3,2,1,0:T(8,128)(2,1)} %cross_spectra.1) | data formatting | bytes 3276800 | tf_op jit(solution)/shard_map/cross_spectra/pallas_call | solution.py:559

commit v2 on v1

v2 whole, which is shorter than its diff:
```python
import functools
import math

import jax
import jax.numpy as jnp
import numpy as np
from jax import lax
from jax.experimental import pallas as pl
from jax.experimental.pallas import tpu as pltpu
from jax.sharding import PartitionSpec as P

NW = 16
WIN = 500
NB = 20
VS = 640
TAPS = 64
DECIM = 4
CH = 128
ROWS = DECIM * NW * WIN
OUTS = NW * WIN
MB = 112
KB = 512
STEP = DECIM * MB
PAIRS = 36
HALO = 64
RAW_PAD = HALO + 2 * PAIRS * STEP
DEC_PAD = 2 * PAIRS * MB
EB = 256
EN_PAD = 8192
CHUNKS = (0, 7168, 13440, 19712, 25984, ROWS)
DR = 48
WITHIN = MB + 4 * DR
MAIN = 16
AR = 40
SR = 56
QR = 400
SHARE = 160
HR = QR // 2
FR = 104
FORGET = math.exp(-1.0 / WIN)
F32 = jnp.float32
BF16 = jnp.bfloat16
MESH = pl.DeviceIdType.MESH


def lowpass_taps():
    offsets = np.arange(TAPS) - (TAPS - 1) / 2.0
    window = 0.54 - 0.46 * np.cos(2.0 * np.pi * np.arange(TAPS) / (TAPS - 1))
    angles = np.pi * 0.8 * offsets / DECIM
    values = np.sin(angles) / angles * window
    return values / values.sum()


def table():
    taps = lowpass_taps()
    lag = DECIM * np.arange(MB)[:, None] + DECIM - 1 + HALO - np.arange(KB)[None, :]
    decim = np.where((lag >= 0) & (lag < TAPS), taps[np.clip(lag, 0, TAPS - 1)], 0.0)
    gap = np.arange(EB)[:, None] - np.arange(EB)[None, :]
    within = np.where(gap >= 0, (1.0 - FORGET) * FORGET ** np.maximum(gap, 0), 0.0)
    phases = 2.0 * np.pi * np.arange(1, NB + 1)[:, None] * np.arange(WIN)[None, :] / WIN
    cos, sin = np.cos(phases) / np.sqrt(WIN), -np.sin(phases) / np.sqrt(WIN)
    ordered = np.concatenate([cos[:MAIN], sin[:MAIN], cos[MAIN:], sin[MAIN:]], axis=0)
    dft = np.zeros((4, DR, 512))
    for place in range(4):
        dft[place, : 2 * NB, 4 * place : 4 * place + WIN] = ordered
    halves = np.concatenate([within[: EB // 2], within[EB // 2 :]], axis=1)
    return jnp.asarray(np.concatenate([decim, dft.reshape(4 * DR, 512), halves], axis=0), BF16)


def kernel(
    blocks_hbm, band_hbm, raw_ref, table_hbm, out_ref,
    blocks_ref, band_ref, table_v, raw_v, dec_v, en_v, run_v, norm_v, white_v, total_v, totals_v,
    own_v, first_v, share_v, shares_v, rows_v, pieces_v, rising_v, weights_v,
    small_sem, raw_sem, halo_sem, tot_sem, a_sem, b_sem, own_ssem, own_rsem, hand_sem, q_ssem, q_rsem,
):
    tm = lax.axis_index("tm")
    chan = lax.axis_index("chan")
    zl, core = tm // 2, tm % 2
    zh, pid = chan // 16, chan % 16
    y, x = pid // 4, pid % 4
    line = zh * 8 + tm
    totals_v[...] = jnp.zeros(totals_v.shape, F32)

    def repeat(count, step):
        lax.fori_loop(0, count, lambda n, carry: (step(n), carry)[1], 0)

    def plane_device(other):
        return (tm, zh * 16 + other)

    def line_device(other):
        return (other % 8, (other // 8) * 16 + pid)

    barrier = pltpu.get_barrier_semaphore()

    def greet(n):
        pl.semaphore_signal(
            barrier, inc=1, device_id=line_device((line + n + 1) % 16), device_id_type=MESH
        )
        pl.semaphore_signal(
            barrier, inc=1, device_id=plane_device((pid + n + 1) % 16), device_id_type=MESH
        )

    repeat(15, greet)

    def chunk(c):
        first, last = CHUNKS[c], CHUNKS[c + 1]
        return pltpu.make_async_copy(
            raw_ref.at[pl.ds(first, last - first)],
            raw_v.at[pl.ds(HALO + first, last - first)],
            raw_sem.at[c],
        )

    small = [
        pltpu.make_async_copy(source, target, small_sem.at[n])
        for n, (source, target) in enumerate(
            ((table_hbm, table_v), (blocks_hbm, blocks_ref), (band_hbm, band_ref))
        )
    ]
    small[0].start()
    for c in range(5):
        chunk(c).start()
    small[1].start()
    small[2].start()
    raw_v[HALO + ROWS : RAW_PAD, :] = jnp.zeros((RAW_PAD - HALO - ROWS, CH), BF16)
    en_v[DEC_PAD:EN_PAD, :] = jnp.zeros((EN_PAD - DEC_PAD, CH), BF16)
    dec_v[DEC_PAD:EN_PAD, :] = jnp.zeros((EN_PAD - DEC_PAD, CH), F32)

    @pl.when(tm == 0)
    def _():
        raw_v[0:HALO, :] = jnp.zeros((HALO, CH), BF16)

    def halo_to(other):
        return pltpu.make_async_remote_copy(
            src_ref=raw_ref.at[pl.ds(ROWS - HALO, HALO)],
            dst_ref=raw_v.at[pl.ds(0, HALO)],
            send_sem=halo_sem.at[0],
            recv_sem=halo_sem.at[1],
            device_id=(other, chan),
            device_id_type=MESH,
        )

    tail = OUTS - (2 * PAIRS - 1) * MB
    back = lax.broadcasted_iota(jnp.int32, (MB, CH), 0).astype(F32) - (MB - 1.0)
    weights_v[0] = (1.0 - FORGET) * jnp.exp(back * (1.0 / WIN))
    back = back + float(MB - tail)
    weights_v[1] = jnp.where(
        back <= 0.0, (1.0 - FORGET) * jnp.exp(jnp.minimum(back, 0.0) * (1.0 / WIN)), 0.0
    )
    place = lax.broadcasted_iota(jnp.int32, (EB, CH), 0).astype(F32)
    rising_v[...] = jnp.exp((place + 1.0) * (-1.0 / WIN))
    small[0].wait()

    block_fade = FORGET**MB
    tail_fade = FORGET**tail

    def decimate(n, total):
        pair = (n + 1) % PAIRS
        is_tail, is_first = pair == PAIRS - 1, pair == 0
        start = pl.multiple_of(pair * (2 * STEP), 128)
        left = raw_v[pl.ds(start, KB), :]
        right = raw_v[pl.ds(start + STEP, KB), :]
        both = jnp.dot(
            table_v[0:MB, :], jnp.concatenate([left, right], axis=1), preferred_element_type=F32
        )
        row = pl.multiple_of(pair * (2 * MB), 32)
        sums = []
        for half in range(2):
            values = both[:, half * CH : (half + 1) * CH]
            dec_v[pl.ds(row + half * MB, MB), :] = values
            energy = values * values
            en_v[pl.ds(row + half * MB, MB), :] = energy.astype(BF16)
            weights = weights_v[0] if half == 0 else weights_v[pair // (PAIRS - 1)]
            sums.append(jnp.sum((weights * energy).reshape(MB // 8, 8, CH), axis=0))
        fade = jnp.where(is_tail, tail_fade, block_fade).astype(F32)
        decay = jnp.where(is_first, 1.0, block_fade * fade).astype(F32)
        gain = jnp.where(is_first, FORGET ** (OUTS - 2 * MB), 1.0).astype(F32)
        return total * decay + (sums[0] * fade + sums[1]) * gain

    def stretch(c, total):
        for n in range(5):

            @pl.when(c == n)
            def _():
                chunk(n).wait()

        @pl.when(c == 4)
        def _():
            pl.semaphore_wait(barrier, 30)

            @pl.when(tm < 7)
            def _():
                halo_to(tm + 1).start()

        @pl.when((c == 5) & (tm > 0))
        def _():
            halo_to(tm - 1).wait_recv()

        return lax.fori_loop(7 * c, 7 * c + 7 - 6 * (c // 5), decimate, total)

    total = lax.fori_loop(0, 6, stretch, jnp.zeros((8, CH), F32))
    total_v[...] = jnp.broadcast_to(jnp.sum(total, axis=0, keepdims=True), (8, CH))

    def total_to(other):
        return pltpu.make_async_remote_copy(
            src_ref=total_v,
            dst_ref=totals_v.at[tm],
            send_sem=tot_sem.at[0],
            recv_sem=tot_sem.at[1],
            device_id=(other, chan),
            device_id_type=MESH,
        )

    repeat(7, lambda n: total_to((tm + n + 1) % 8).start())

    def arrived(ref, sem):
        pltpu.make_async_remote_copy(
            src_ref=ref, dst_ref=ref, send_sem=sem, recv_sem=sem,
            device_id=plane_device((pid + 1) % 16), device_id_type=MESH,
        ).wait_recv()

    def departed(ref, sem):
        pltpu.make_async_remote_copy(
            src_ref=ref, dst_ref=ref, send_sem=sem, recv_sem=sem,
            device_id=plane_device((pid + 1) % 16), device_id_type=MESH,
        ).wait_send()

    halves = table_v[WITHIN : WITHIN + EB // 2, :]
    within = jnp.concatenate([halves[:, :EB], halves[:, EB:]], axis=0)

    def local_run(n):
        row = pl.multiple_of(n * (2 * EB), 2 * EB)
        rhs = jnp.concatenate([en_v[pl.ds(row, EB), :], en_v[pl.ds(row + EB, EB), :]], axis=1)
        both = jnp.dot(within, rhs, preferred_element_type=F32)
        run_v[pl.ds(row, EB), :] = both[:, :CH]
        run_v[pl.ds(row + EB, EB), :] = both[:, CH:]

    repeat(EN_PAD // (2 * EB), local_run)
    arrived(totals_v.at[pl.ds(0, 7)], tot_sem.at[1])

    state = jnp.zeros((8, CH), F32)
    for group in range(7):
        state = jnp.where(group < tm, state * math.exp(-NW) + totals_v[group], state)

    def normalize(block, state):
        row = pl.multiple_of(block * EB, EB)
        running = run_v[pl.ds(row, EB), :] + rising_v[...] * state[0:1, :]
        values = dec_v[pl.ds(row, EB), :] * lax.rsqrt(jnp.maximum(running, 0.01))
        norm_v[pl.ds(row, EB), :] = values.astype(BF16)
        return jnp.broadcast_to(running[EB - 1 : EB, :], (8, CH))

    lax.fori_loop(0, OUTS // EB + 1, normalize, state)

    small[1].wait()
    small[2].wait()
    low, high = band_ref[0], band_ref[1]
    row_id = lax.broadcasted_iota(jnp.int32, (2 * NB, CH), 0)
    bin_id = jnp.where(row_id < 2 * MAIN, row_id % MAIN, MAIN + row_id % 4)
    keep = jnp.where((bin_id >= low) & (bin_id < high), 1.0, 0.0).astype(F32)

    def spectra_of(n):
        first = n + n // 4 * 4
        start = pl.multiple_of(first * WIN // 16 * 16, 16)
        rhs = jnp.concatenate(
            [norm_v[pl.ds(start, 512), :], norm_v[pl.ds(start + 4 * WIN, 512), :]], axis=1
        )
        part = pl.multiple_of(MB + first * WIN % 16 // 4 * DR, 16)
        both = jnp.dot(table_v[pl.ds(part, DR), :], rhs, preferred_element_type=F32)
        for half in range(2):
            w = first + 4 * half
            spectra = both[: 2 * NB, half * CH : (half + 1) * CH]
            power = jnp.sum(spectra * spectra, axis=0, keepdims=True) / NB
            white = spectra * keep * lax.rsqrt(jnp.maximum(power, 0.1))
            for p in range(2):
                white_v[pl.ds(p * NW + w, MAIN, stride=AR), :] = white[p * MAIN : (p + 1) * MAIN]
                white_v[pl.ds(w // 4 * (4 * AR) + 32 + p * 4 + w % 4, 4, stride=AR), :] = white[
                    32 + 4 * p : 36 + 4 * p
                ]

    repeat(8, spectra_of)
    own_v[tm] = white_v[...].reshape(MAIN, AR, CH).astype(BF16)

    def plane_copy(other):
        return pltpu.make_async_remote_copy(
            src_ref=own_v.at[tm, other],
            dst_ref=first_v.at[pid],
            send_sem=a_sem.at[0],
            recv_sem=a_sem.at[1],
            device_id=plane_device(other),
            device_id_type=MESH,
        )

    repeat(15, lambda n: plane_copy((pid + n + 1) % 16).start())

    def own_copy(group, other, slot, arrival):
        return pltpu.make_async_remote_copy(
            src_ref=own_v.at[group],
            dst_ref=own_v.at[group],
            send_sem=own_ssem.at[slot],
            recv_sem=arrival,
            device_id=(other, chan),
            device_id_type=MESH,
        )

    partner = zl * 2 + 1 - core

    def hand_over(group):
        return pltpu.make_async_remote_copy(
            src_ref=own_v.at[group],
            dst_ref=own_v.at[group],
            send_sem=hand_sem.at[0],
            recv_sem=hand_sem.at[1],
            device_id=(partner, chan),
            device_id_type=MESH,
        )

    sends = []

    def send_along(condition, group, other, slot):
        sends.append((condition, group, other, slot))

        @pl.when(condition)
        def _():
            own_copy(group, other, slot, own_rsem.at[group // 2]).start()

    send_along(zl < 3, tm, tm + 2, 0)
    send_along(zl > 0, tm, tm - 2, 1)
    hand_over(tm).start()

    def relay_own(step):
        below, above = tm - 2 * step, tm + 2 * step

        @pl.when(zl - step >= 0)
        def _():
            own_copy(below, partner, 0, own_rsem.at[below // 2]).wait_recv()

        @pl.when(zl + step <= 3)
        def _():
            own_copy(above, partner, 0, own_rsem.at[above // 2]).wait_recv()

        if step < 3:
            send_along((zl - step >= 0) & (zl < 3), below, tm + 2, 2 * step)
            send_along((zl + step <= 3) & (zl > 0), above, tm - 2, 2 * step + 1)

        @pl.when(zl - step >= 0)
        def _():
            hand_over(below).start()

        @pl.when(zl + step <= 3)
        def _():
            hand_over(above).start()

    first_v[pid] = own_v[tm, pid]
    arrived(first_v.at[pl.ds(0, 15)], a_sem.at[1])

    lane8 = lax.broadcasted_iota(jnp.int32, (8, CH), 1)
    lane40 = lax.broadcasted_iota(jnp.int32, (AR, CH), 1)

    def cut_share(share):
        jj = share % 4
        two = []
        for i in range(2):
            block = blocks_ref[share // 4] + jj + i
            here = jnp.where(block // 16 == zh, 1.0, 0.0).astype(F32)
            two.append(first_v[block % 16].astype(F32) * here)
        a, c = two
        turn = CH - 32 * jj
        head = jnp.where(
            lane40 < turn, pltpu.roll(a, turn % CH, axis=1), pltpu.roll(c, turn % CH, axis=1)
        )
        turned = pltpu.roll(c, (CH - 32 * jj) % CH, axis=1)
        rest = jnp.where(lane8 < 32, turned[0:8], 0.0)
        for q in range(1, 4):
            part = pltpu.roll(turned[8 * q : 8 * q + 8], 32 * q, axis=1)
            rest = jnp.where((lane8 >= 32 * q) & (lane8 < 32 * q + 32), part, rest)
        last_rest = jnp.where(lane8 < 32, turned[32:40], 0.0)
        share_v[share] = jnp.concatenate([head, rest, last_rest], axis=0).astype(BF16)

    repeat(8, cut_share)

    def line_copy(other):
        return pltpu.make_async_remote_copy(
            src_ref=share_v.at[other % 8],
            dst_ref=shares_v.at[line],
            send_sem=b_sem.at[0],
            recv_sem=b_sem.at[1],
            device_id=line_device(other),
            device_id_type=MESH,
        )

    repeat(15, lambda n: line_copy((line + n + 1) % 16).start())
    shares_v[line] = share_v[tm]
    relay_own(1)
    arrived(shares_v.at[pl.ds(0, 15)], b_sem.at[1])

    def unpack(g):
        both = shares_v[g].astype(F32) + shares_v[8 + g].astype(F32)
        rests = [both[40:48]]
        for q in range(1, 4):
            rests.append(pltpu.roll(both[40:48], CH - 32 * q, axis=1))
        rests.append(both[48:56])
        rows = jnp.concatenate([both[0:40], jnp.concatenate(rests, axis=0)], axis=1)
        rows_v[pl.ds(pl.multiple_of(g * 32, 32), 32), :] = rows[0:32]
        rows_v[pl.ds(pl.multiple_of(256 + g * 8, 8), 8), :] = rows[32:40]
        rows_v[pl.ds(pl.multiple_of(320 + g * 8, 8), 8), :] = rows[32:40]

    repeat(8, unpack)
    eye = (
        lax.broadcasted_iota(jnp.int32, (SHARE, 256), 0)
        == lax.broadcasted_iota(jnp.int32, (SHARE, 256), 1)
    )
    eye = jnp.where(eye, 1.0, 0.0).astype(BF16)
    turned = lax.dot_general(
        eye, rows_v[...].astype(BF16), (((1,), (1,)), ((), ())), preferred_element_type=F32
    )
    half_lane = lax.broadcasted_iota(jnp.int32, (80, CH), 1) < 64
    packed_tail = jnp.where(half_lane, turned[0:80, 2 * CH :], turned[80:160, 2 * CH :])
    pieces_v[pid] = jnp.concatenate(
        [turned[:, :CH], turned[:, CH : 2 * CH], packed_tail], axis=0
    ).astype(BF16)

    def at(h, f, s):
        dx, dy = f * (1 - h) + s * h, f * h + s * (1 - h)
        return ((y + dy) % 4) * 4 + (x + dx) % 4

    def piece_copy(h, f, s, along, across, first, count, event):
        rows = pl.ds(pl.multiple_of(h * HR + first, 8), count)
        return pltpu.make_async_remote_copy(
            src_ref=pieces_v.at[at(h, f, s), rows],
            dst_ref=pieces_v.at[at(h, f, s), rows],
            send_sem=q_ssem.at[0],
            recv_sem=q_rsem.at[event],
            device_id=plane_device(at(h, along, across)),
            device_id_type=MESH,
        )

    def wait_half(h, f, s, event):
        piece_copy(h, f, s, 1, 0, 0, HR, event).wait_recv()

    def send_across(h, f):
        for t in range(2):
            piece_copy(h, f, 0, 0, 1 + 2 * t, 0, HR, h * 11 + 3 + 2 * f + t).start()

    def forward(h, f, s, along, t, event):
        first, count = ((0, FR), (FR, HR - FR))[t]
        step = 1 + 2 * t
        piece_copy(
            h, f, s, step if along else 0, 0 if along else step, first, count, event
        ).start()

    def own_half(h):
        for t in range(2):
            piece_copy(h, 0, 0, 1 + 2 * t, 0, 0, HR, h * 11 + t).start()

    def near_along(h):
        for t in range(2):
            wait_half(h, 3 - 2 * t, 0, h * 11 + t)
            forward(h, 3 - 2 * t, 0, True, t, h * 11 + 2)
            send_across(h, 3 - 2 * t)

    def near_across(h, f):
        for t in range(2):
            wait_half(h, f, 3 - 2 * t, h * 11 + 3 + 2 * f + t)
            forward(h, f, 3 - 2 * t, False, t, 22)

    def far_along(h):
        wait_half(h, 2, 0, h * 11 + 2)
        send_across(h, 2)

    repeat(2, own_half)
    repeat(2, lambda h: send_across(h, 0))
    repeat(2, near_along)
    repeat(2, lambda h: near_across(h, 0))
    repeat(2, far_along)
    relay_own(2)
    repeat(6, lambda n: near_across(n % 2, n // 2 + 1))
    relay_own(3)
    arrived(own_v.at[pl.ds(0, 4)], hand_sem.at[1])

    scale = 1.0 / math.sqrt(8 * NW)

    def put(k, lhs, rhs):
        both = jnp.dot(lhs, rhs, preferred_element_type=F32) * scale
        out_ref[pl.ds(2 * k, SHARE, stride=2 * NB), :] = both[:, :CH]
        out_ref[pl.ds(2 * k + 1, SHARE, stride=2 * NB), :] = both[:, CH:]

    def main_bin(k):
        lhs = jnp.concatenate([pieces_v[k, 0:SHARE], pieces_v[k, SHARE : 2 * SHARE]], axis=1)
        re, im = [], []
        for g in range(8):
            rows = own_v[g, k, 0:32]
            re.append(rows)
            im.append(rows[16:32])
            im.append(-rows[0:16])
        rhs = jnp.concatenate([jnp.concatenate(re, axis=0), jnp.concatenate(im, axis=0)], axis=1)
        put(k, lhs, rhs)

    def near_bin(n):
        f, s = n % 3, n // 3
        main_bin(at(0, f + f // 2, s + s // 2))

    def far_bin(n):
        late, m = n // 4, n % 4
        main_bin(at(0, 2 * (1 - late) + late * (m + m // 2), m * (1 - late) + 2 * late))

    repeat(9, near_bin)
    arrived(pieces_v.at[pl.ds(0, 4)], q_rsem.at[22])
    repeat(7, far_bin)

    sign = jnp.where(lax.broadcasted_iota(jnp.int32, (8, CH), 0) < 4, 1.0, -1.0).astype(F32)

    def tail_bin(kk):
        columns = []
        for pair in range(2):
            even = pieces_v[pair * 8 + kk, 2 * SHARE : QR].astype(F32)
            odd = pieces_v[pair * 8 + 4 + kk, 2 * SHARE : QR].astype(F32)
            upper = jnp.where(half_lane, even, pltpu.roll(odd, 64, axis=1))
            lower = jnp.where(half_lane, pltpu.roll(even, 64, axis=1), odd)
            columns.append(jnp.concatenate([upper, lower], axis=0))
        lhs = jnp.concatenate(columns, axis=1).astype(BF16)
        re, im = [], []
        for wh in range(4):
            for g in range(8):
                rows = own_v[g, wh * 4 + kk, 32:40].astype(F32)
                re.append(rows)
                im.append(pltpu.roll(rows, 4, axis=0) * sign)
        rhs = jnp.concatenate([jnp.concatenate(re, axis=0), jnp.concatenate(im, axis=0)], axis=1)
        put(MAIN + kk, lhs, rhs.astype(BF16))

    repeat(NB - MAIN, tail_bin)

    @pl.when(tm < 7)
    def _():
        halo_to(tm + 1).wait_send()

    departed(totals_v.at[pl.ds(0, 7)], tot_sem.at[0])
    departed(first_v.at[pl.ds(0, 15)], a_sem.at[0])
    departed(shares_v.at[pl.ds(0, 15)], b_sem.at[0])
    departed(own_v.at[pl.ds(0, 4)], hand_sem.at[0])
    departed(pieces_v.at[pl.ds(0, 15)], q_ssem.at[0])
    for condition, group, other, slot in sends:

        @pl.when(condition)
        def _():
            own_copy(group, other, slot, own_rsem.at[0]).wait_send()


def body(raw_strain, source_blocks, band_bins):
    hbm = pl.BlockSpec(memory_space=pltpu.HBM)
    vmem = pl.BlockSpec(memory_space=pltpu.VMEM)
    dma = pltpu.SemaphoreType.DMA
    rows = pl.pallas_call(
        kernel,
        out_shape=jax.ShapeDtypeStruct((SHARE * NB * 2, CH), F32),
        in_specs=[hbm] * 4,
        out_specs=vmem,
        scratch_shapes=[
            pltpu.SMEM((2,), jnp.int32),
            pltpu.SMEM((2,), jnp.int32),
            pltpu.VMEM((WITHIN + EB // 2, 512), BF16),
            pltpu.VMEM((RAW_PAD, CH), BF16),
            pltpu.VMEM((EN_PAD, CH), F32),
            pltpu.VMEM((EN_PAD, CH), BF16),
            pltpu.VMEM((EN_PAD, CH), F32),
            pltpu.VMEM((EN_PAD, CH), BF16),
            pltpu.VMEM((MAIN * AR, CH), F32),
            pltpu.VMEM((8, CH), F32),
            pltpu.VMEM((8, 8, CH), F32),
            pltpu.VMEM((8, MAIN, AR, CH), BF16),
            pltpu.VMEM((16, AR, CH), BF16),
            pltpu.VMEM((8, SR, CH), BF16),
            pltpu.VMEM((16, SR, CH), BF16),
            pltpu.VMEM((384, 256), F32),
            pltpu.VMEM((16, QR, CH), BF16),
            pltpu.VMEM((EB, CH), F32),
            pltpu.VMEM((2, MB, CH), F32),
            dma((3,)),
            dma((5,)),
            dma((2,)),
            dma((2,)),
            dma((2,)),
            dma((2,)),
            dma((6,)),
            dma((4,)),
            dma((2,)),
            dma((1,)),
            dma((23,)),
        ],
        compiler_params=pltpu.CompilerParams(
            collective_id=0, has_side_effects=True, vmem_limit_bytes=50 * 2**20
        ),
        name="cross_spectra",
    )(source_blocks, band_bins, raw_strain, table())
    return rows.reshape(SHARE, NB, 2, CH).transpose(0, 2, 1, 3).astype(BF16)


def solution(mesh):
    in_specs = (P("tm", "chan"), P(), P())
    out_specs = P("tm", None, None, "chan")
    return jax.shard_map(body, mesh=mesh, in_specs=in_specs, out_specs=out_specs, check_vma=False)
```

time: 77.9 us -> 61.1 us (0.78)
  the two profiles are of different devices: /device:TPU:4 before, /device:TPU:1 now
where the time goes in v2:
time: 61.1 us; the launch traced here: 61 us
  Pallas kernels  57.3 us (94%)
  local copies, waits for them, and re-layouts  2.32 us (4%)
  other arithmetic  1.32 us (2%)
    pallas_call x1, Pallas kernels, body(): pl.pallas_call(kernel, out_shape=jax.ShapeDtypeStruct((SHARE * NB * 2, CH...  57.3 us
    unnamed x6, local copies, waits for them, and re-layouts  2.32 us
    convert_element_type x1, other arithmetic, body(): return rows.reshape(SHARE, NB, 2, CH).transpose(0, 2, 1, 3).astype(BF16)  1.32 us

profile of v2, /device:TPU:1, one launch (start us, length us, event | category | flops | bytes accessed | tf_op | source)
XLA Modules:
  0.0 61.0 jit_solution(8592299374364552649)
XLA Ops:
  0.0 0.0 copy-start
  0.0 1.0 %copy-done = bf16[432,512]{1,0:T(8,128)(2,1)S(1)} copy-done((bf16[432,512]{1,0:T(8,128)(2,1)S(1)}, bf16[432,512]{1,0:T(8,128)(2,1)}, u32[]{:S(2)}) %copy-start) | copy-done | bytes 442392
  1.0 0.0 copy-start.1
  1.0 0.7 %copy-done.1 = s32[2]{0:T(128)S(1)} copy-done((s32[2]{0:T(128)S(1)}, s32[2]{0:T(128)}, u32[]{:S(2)}) %copy-start.1) | copy-done | bytes 32
  1.7 0.0 copy-start.2
  1.7 0.7 %copy-done.2 = s32[2]{0:T(128)S(1)} copy-done((s32[2]{0:T(128)S(1)}, s32[2]{0:T(128)}, u32[]{:S(2)}) %copy-start.2) | copy-done | bytes 32
  2.3 57.3 %cross_spectra.1 = f32[6400,128]{1,0:T(8,128)S(1)} custom-call(s32[2]{0:T(128)S(1)} %copy-done.1, s32[2]{0:T(128)S(1)} %copy-done.2, bf16[32000,128]{1,0:T(8,128)(2,1)} %raw_ref.1, bf16[432,512]{1,0:T(8,128)(2,1)S(1)} %copy-done), custom_call_target="tpu_custom_call" | custom-call | tf_op jit(solution)/shard_map/cross_spectra/pallas_call | solution.py:551
  59.7 1.3 %convert_element_type.9 = bf16[6400,128]{1,0:T(8,128)(2,1)} convert(f32[6400,128]{1,0:T(8,128)S(1)} %cross_spectra.1) | non-fusion elementwise | flops 819200 | bytes 4915200 | tf_op jit(solution)/shard_map/convert_element_type | solution.py:593
Async XLA Ops:
  0.0 1.0 %copy-start = (bf16[432,512]{1,0:T(8,128)(2,1)S(1)}, bf16[432,512]{1,0:T(8,128)(2,1)}, u32[]{:S(2)}) copy-start(bf16[432,512]{1,0:T(8,128)(2,1)} %constant.2.clone.table_hbm) | copy-start | bytes 1327108
  1.0 0.7 %copy-start.1 = (s32[2]{0:T(128)S(1)}, s32[2]{0:T(128)}, u32[]{:S(2)}) copy-start(s32[2]{0:T(128)} %blocks_hbm.1) | copy-start | bytes 28
  1.7 0.7 %copy-start.2 = (s32[2]{0:T(128)S(1)}, s32[2]{0:T(128)}, u32[]{:S(2)}) copy-start(s32[2]{0:T(128)} %band_hbm.1) | copy-start | bytes 28

commit v3 on v2

--- a/solution.py
+++ b/solution.py
@@ -27,15 +27,18 @@
 DEC_PAD = 2 * PAIRS * MB
 EB = 256
 EN_PAD = 8192
-CHUNKS = (0, 7168, 13440, 19712, 25984, ROWS)
+CHUNKS = (0, 6272, 11648, 17024, 22400, 27776, ROWS)
 DR = 48
-WITHIN = MB + 4 * DR
 MAIN = 16
 AR = 40
 SR = 56
 QR = 400
 SHARE = 160
 HR = QR // 2
+FAR_FIRST = sorted(
+    ((dy, dx) for dy in range(4) for dx in range(4) if dy or dx),
+    key=lambda step: (-min(step[0], 4 - step[0]) - min(step[1], 4 - step[1]), step),
+)
 FR = 104
 FORGET = math.exp(-1.0 / WIN)
 F32 = jnp.float32
@@ -51,25 +54,57 @@
     return values / values.sum()
 
 
-def table():
-    taps = lowpass_taps()
-    lag = DECIM * np.arange(MB)[:, None] + DECIM - 1 + HALO - np.arange(KB)[None, :]
-    decim = np.where((lag >= 0) & (lag < TAPS), taps[np.clip(lag, 0, TAPS - 1)], 0.0)
-    gap = np.arange(EB)[:, None] - np.arange(EB)[None, :]
-    within = np.where(gap >= 0, (1.0 - FORGET) * FORGET ** np.maximum(gap, 0), 0.0)
-    phases = 2.0 * np.pi * np.arange(1, NB + 1)[:, None] * np.arange(WIN)[None, :] / WIN
-    cos, sin = np.cos(phases) / np.sqrt(WIN), -np.sin(phases) / np.sqrt(WIN)
-    ordered = np.concatenate([cos[:MAIN], sin[:MAIN], cos[MAIN:], sin[MAIN:]], axis=0)
-    dft = np.zeros((4, DR, 512))
+def make_tables(table_v, filter_v, within_v):
+    taps = lowpass_taps().astype(jnp.bfloat16).astype(np.float32)
+    row = lax.broadcasted_iota(jnp.int32, (8, CH), 0)
+    lane = lax.broadcasted_iota(jnp.int32, (8, CH), 1)
+    lag = DECIM * row + DECIM - 1 + HALO - lane
+    eight = jnp.zeros((8, CH), F32)
+    for j in range(TAPS):
+        eight = jnp.where(lag == j, float(taps[j]), eight)
+    for b in range(MB // 16):
+        rows = []
+        for half in range(2):
+            shift = 32 * (2 * b + half)
+            turned = pltpu.roll(eight, shift % CH, axis=1) if shift % CH else eight
+            columns = []
+            for q in range(KB // CH):
+                if q == shift // CH:
+                    columns.append(jnp.where(lane >= shift % CH, turned, 0.0))
+                elif q == shift // CH + 1:
+                    columns.append(jnp.where(lane < shift % CH, turned, 0.0))
+                else:
+                    columns.append(jnp.zeros((8, CH), F32))
+            rows.append(jnp.concatenate(columns, axis=1))
+        filter_v[16 * b : 16 * b + 16, :] = jnp.concatenate(rows, axis=0).astype(BF16)
+    gap = lax.broadcasted_iota(jnp.int32, (EB, EB), 0) - lax.broadcasted_iota(jnp.int32, (EB, EB), 1)
+    share = (1.0 - FORGET) * jnp.exp(jnp.maximum(gap, 0).astype(F32) * (-1.0 / WIN))
+    within_v[...] = jnp.where(gap >= 0, share, 0.0).astype(BF16)
+    row = lax.broadcasted_iota(jnp.int32, (DR, 512), 0)
+    time = lax.broadcasted_iota(jnp.int32, (DR, 512), 1)
+    late = row >= 2 * MAIN
+    bin_id = jnp.where(late, MAIN + row % 4, row % MAIN)
+    quarter = jnp.where(late, row // 4 % 2, row // MAIN % 2)
+    angle = ((bin_id + 1) * time + (WIN // 4) * quarter).astype(F32)
+    angle = angle - jnp.floor(angle * (1.0 / WIN)) * WIN
+    angle = jnp.where(angle < 0.0, angle + WIN, jnp.where(angle >= WIN, angle - WIN, angle))
+    angle = jnp.minimum(angle, WIN - angle)
+    flip = angle > WIN / 4.0
+    angle = jnp.where(flip, WIN / 2.0 - angle, angle)
+    square = (angle * angle) * ((2.0 * math.pi / WIN) ** 2)
+    cosine = jnp.full((DR, 512), 1.0, F32)
+    for order in (14, 12, 10, 8, 6, 4, 2):
+        cosine = 1.0 - square * cosine * (1.0 / (order * (order - 1)))
+    cosine = jnp.where(flip, -cosine, cosine) * (1.0 / math.sqrt(WIN))
+    cosine = jnp.where((time < WIN) & (row < 2 * NB), cosine, 0.0)
     for place in range(4):
-        dft[place, : 2 * NB, 4 * place : 4 * place + WIN] = ordered
-    halves = np.concatenate([within[: EB // 2], within[EB // 2 :]], axis=1)
-    return jnp.asarray(np.concatenate([decim, dft.reshape(4 * DR, 512), halves], axis=0), BF16)
+        shifted = pltpu.roll(cosine, 4 * place, axis=1) if place else cosine
+        table_v[place] = shifted.astype(BF16)
 
 
 def kernel(
-    blocks_hbm, band_hbm, raw_ref, table_hbm, out_ref,
-    blocks_ref, band_ref, table_v, raw_v, dec_v, en_v, run_v, norm_v, white_v, total_v, totals_v,
+    blocks_hbm, band_hbm, raw_ref, out_ref,
+    blocks_ref, band_ref, table_v, filter_v, within_v, raw_v, dec_v, en_v, run_v, norm_v, white_v, total_v, totals_v,
     own_v, first_v, share_v, shares_v, rows_v, pieces_v, rising_v, weights_v,
     small_sem, raw_sem, halo_sem, tot_sem, a_sem, b_sem, own_ssem, own_rsem, hand_sem, q_ssem, q_rsem,
 ):
@@ -84,6 +119,10 @@
     def repeat(count, step):
         lax.fori_loop(0, count, lambda n, carry: (step(n), carry)[1], 0)
 
+    def unrolled(count, step):
+        for n in range(count):
+            step(n)
+
     def plane_device(other):
         return (tm, zh * 16 + other)
 
@@ -113,14 +152,13 @@
     small = [
         pltpu.make_async_copy(source, target, small_sem.at[n])
         for n, (source, target) in enumerate(
-            ((table_hbm, table_v), (blocks_hbm, blocks_ref), (band_hbm, band_ref))
+            ((blocks_hbm, blocks_ref), (band_hbm, band_ref))
         )
     ]
+    for c in range(6):
+        chunk(c).start()
     small[0].start()
-    for c in range(5):
-        chunk(c).start()
     small[1].start()
-    small[2].start()
     raw_v[HALO + ROWS : RAW_PAD, :] = jnp.zeros((RAW_PAD - HALO - ROWS, CH), BF16)
     en_v[DEC_PAD:EN_PAD, :] = jnp.zeros((EN_PAD - DEC_PAD, CH), BF16)
     dec_v[DEC_PAD:EN_PAD, :] = jnp.zeros((EN_PAD - DEC_PAD, CH), F32)
@@ -148,7 +186,7 @@
     )
     place = lax.broadcasted_iota(jnp.int32, (EB, CH), 0).astype(F32)
     rising_v[...] = jnp.exp((place + 1.0) * (-1.0 / WIN))
-    small[0].wait()
+    make_tables(table_v, filter_v, within_v)
 
     block_fade = FORGET**MB
     tail_fade = FORGET**tail
@@ -160,7 +198,7 @@
         left = raw_v[pl.ds(start, KB), :]
         right = raw_v[pl.ds(start + STEP, KB), :]
         both = jnp.dot(
-            table_v[0:MB, :], jnp.concatenate([left, right], axis=1), preferred_element_type=F32
+            filter_v[...], jnp.concatenate([left, right], axis=1), preferred_element_type=F32
         )
         row = pl.multiple_of(pair * (2 * MB), 32)
         sums = []
@@ -176,8 +214,11 @@
         gain = jnp.where(is_first, FORGET ** (OUTS - 2 * MB), 1.0).astype(F32)
         return total * decay + (sums[0] * fade + sums[1]) * gain
 
+    def two_pairs(n, total):
+        return decimate(n + 1, decimate(n, total))
+
     def stretch(c, total):
-        for n in range(5):
+        for n in range(6):
 
             @pl.when(c == n)
             def _():
@@ -195,7 +236,7 @@
         def _():
             halo_to(tm - 1).wait_recv()
 
-        return lax.fori_loop(7 * c, 7 * c + 7 - 6 * (c // 5), decimate, total)
+        return lax.fori_loop(0, 3, lambda n, t: two_pairs(6 * c + 2 * n, t), total)
 
     total = lax.fori_loop(0, 6, stretch, jnp.zeros((8, CH), F32))
     total_v[...] = jnp.broadcast_to(jnp.sum(total, axis=0, keepdims=True), (8, CH))
@@ -224,13 +265,10 @@
             device_id=plane_device((pid + 1) % 16), device_id_type=MESH,
         ).wait_send()
 
-    halves = table_v[WITHIN : WITHIN + EB // 2, :]
-    within = jnp.concatenate([halves[:, :EB], halves[:, EB:]], axis=0)
-
     def local_run(n):
         row = pl.multiple_of(n * (2 * EB), 2 * EB)
         rhs = jnp.concatenate([en_v[pl.ds(row, EB), :], en_v[pl.ds(row + EB, EB), :]], axis=1)
-        both = jnp.dot(within, rhs, preferred_element_type=F32)
+        both = jnp.dot(within_v[...], rhs, preferred_element_type=F32)
         run_v[pl.ds(row, EB), :] = both[:, :CH]
         run_v[pl.ds(row + EB, EB), :] = both[:, CH:]
 
@@ -250,8 +288,8 @@
 
     lax.fori_loop(0, OUTS // EB + 1, normalize, state)
 
+    small[0].wait()
     small[1].wait()
-    small[2].wait()
     low, high = band_ref[0], band_ref[1]
     row_id = lax.broadcasted_iota(jnp.int32, (2 * NB, CH), 0)
     bin_id = jnp.where(row_id < 2 * MAIN, row_id % MAIN, MAIN + row_id % 4)
@@ -259,12 +297,11 @@
 
     def spectra_of(n):
         first = n + n // 4 * 4
-        start = pl.multiple_of(first * WIN // 16 * 16, 16)
+        start = first * WIN // 16 * 16
         rhs = jnp.concatenate(
             [norm_v[pl.ds(start, 512), :], norm_v[pl.ds(start + 4 * WIN, 512), :]], axis=1
         )
-        part = pl.multiple_of(MB + first * WIN % 16 // 4 * DR, 16)
-        both = jnp.dot(table_v[pl.ds(part, DR), :], rhs, preferred_element_type=F32)
+        both = jnp.dot(table_v[first * WIN % 16 // 4], rhs, preferred_element_type=F32)
         for half in range(2):
             w = first + 4 * half
             spectra = both[: 2 * NB, half * CH : (half + 1) * CH]
@@ -276,7 +313,7 @@
                     32 + 4 * p : 36 + 4 * p
                 ]
 
-    repeat(8, spectra_of)
+    unrolled(8, spectra_of)
     own_v[tm] = white_v[...].reshape(MAIN, AR, CH).astype(BF16)
 
     def plane_copy(other):
@@ -289,7 +326,8 @@
             device_id_type=MESH,
         )
 
-    repeat(15, lambda n: plane_copy((pid + n + 1) % 16).start())
+    for dy, dx in FAR_FIRST:
+        plane_copy((y + dy) % 4 * 4 + (x + dx) % 4).start()
 
     def own_copy(group, other, slot, arrival):
         return pltpu.make_async_remote_copy(
@@ -355,27 +393,26 @@
     lane8 = lax.broadcasted_iota(jnp.int32, (8, CH), 1)
     lane40 = lax.broadcasted_iota(jnp.int32, (AR, CH), 1)
 
-    def cut_share(share):
+    def turn_left(rows, lanes):
+        return pltpu.roll(rows, CH - lanes, axis=1) if lanes else rows
+
+    picked = []
+    for b in range(2):
+        for i in range(5):
+            block = blocks_ref[b] + i
+            here = jnp.where(block // 16 == zh, 1.0, 0.0).astype(F32)
+            picked.append(first_v[block % 16].astype(F32) * here)
+    for share in range(8):
         jj = share % 4
-        two = []
-        for i in range(2):
-            block = blocks_ref[share // 4] + jj + i
-            here = jnp.where(block // 16 == zh, 1.0, 0.0).astype(F32)
-            two.append(first_v[block % 16].astype(F32) * here)
-        a, c = two
-        turn = CH - 32 * jj
-        head = jnp.where(
-            lane40 < turn, pltpu.roll(a, turn % CH, axis=1), pltpu.roll(c, turn % CH, axis=1)
-        )
-        turned = pltpu.roll(c, (CH - 32 * jj) % CH, axis=1)
+        a, c = picked[share // 4 * 5 + jj], picked[share // 4 * 5 + jj + 1]
+        turned = turn_left(c, 32 * jj)
+        head = jnp.where(lane40 < CH - 32 * jj, turn_left(a, 32 * jj), turned)
         rest = jnp.where(lane8 < 32, turned[0:8], 0.0)
         for q in range(1, 4):
             part = pltpu.roll(turned[8 * q : 8 * q + 8], 32 * q, axis=1)
             rest = jnp.where((lane8 >= 32 * q) & (lane8 < 32 * q + 32), part, rest)
         last_rest = jnp.where(lane8 < 32, turned[32:40], 0.0)
         share_v[share] = jnp.concatenate([head, rest, last_rest], axis=0).astype(BF16)
-
-    repeat(8, cut_share)
 
     def line_copy(other):
         return pltpu.make_async_remote_copy(
@@ -387,7 +424,10 @@
             device_id_type=MESH,
         )
 
-    repeat(15, lambda n: line_copy((line + n + 1) % 16).start())
+    for dz in (4, 3, 5, 2, 6, 1, 7):
+        for dc in range(2):
+            line_copy((line // 2 + dz) % 8 * 2 + (core + dc) % 2).start()
+    line_copy(line + 1 - 2 * core).start()
     shares_v[line] = share_v[tm]
     relay_own(1)
     arrived(shares_v.at[pl.ds(0, 15)], b_sem.at[1])
@@ -403,7 +443,7 @@
         rows_v[pl.ds(pl.multiple_of(256 + g * 8, 8), 8), :] = rows[32:40]
         rows_v[pl.ds(pl.multiple_of(320 + g * 8, 8), 8), :] = rows[32:40]
 
-    repeat(8, unpack)
+    unrolled(8, unpack)
     eye = (
         lax.broadcasted_iota(jnp.int32, (SHARE, 256), 0)
         == lax.broadcasted_iota(jnp.int32, (SHARE, 256), 1)
@@ -551,12 +591,14 @@
     rows = pl.pallas_call(
         kernel,
         out_shape=jax.ShapeDtypeStruct((SHARE * NB * 2, CH), F32),
-        in_specs=[hbm] * 4,
+        in_specs=[hbm] * 3,
         out_specs=vmem,
         scratch_shapes=[
             pltpu.SMEM((2,), jnp.int32),
             pltpu.SMEM((2,), jnp.int32),
-            pltpu.VMEM((WITHIN + EB // 2, 512), BF16),
+            pltpu.VMEM((4, DR, 512), BF16),
+            pltpu.VMEM((MB, KB), BF16),
+            pltpu.VMEM((EB, EB), BF16),
             pltpu.VMEM((RAW_PAD, CH), BF16),
             pltpu.VMEM((EN_PAD, CH), F32),
             pltpu.VMEM((EN_PAD, CH), BF16),
@@ -573,8 +615,8 @@
             pltpu.VMEM((16, QR, CH), BF16),
             pltpu.VMEM((EB, CH), F32),
             pltpu.VMEM((2, MB, CH), F32),
-            dma((3,)),
-            dma((5,)),
+            dma((2,)),
+            dma((6,)),
             dma((2,)),
             dma((2,)),
             dma((2,)),
@@ -589,7 +631,7 @@
             collective_id=0, has_side_effects=True, vmem_limit_bytes=50 * 2**20
         ),
         name="cross_spectra",
-    )(source_blocks, band_bins, raw_strain, table())
+    )(source_blocks, band_bins, raw_strain)
     return rows.reshape(SHARE, NB, 2, CH).transpose(0, 2, 1, 3).astype(BF16)
 
 

time: 61.1 us -> 54 us (0.88)
  Pallas kernels: 57.3 us -> 51.2 us
  local copies, waits for them, and re-layouts: 2.32 us -> 1.31 us
    pallas_call x1, Pallas kernels: 57.3 us -> 51.2 us  [body(): pl.pallas_call(kernel, out_shape=jax.ShapeDtypeStruct((SHARE * NB * 2, CH...]
    unnamed x6 -> x4, local copies, waits for them, and re-layouts: 2.32 us -> 1.31 us
where the time goes in v3:
time: 54 us; the launch traced here: 53.9 us
  Pallas kernels  51.2 us (95%)
  other arithmetic  1.32 us (2%)
  local copies, waits for them, and re-layouts  1.31 us (2%)
    pallas_call x1, Pallas kernels, body(): pl.pallas_call(kernel, out_shape=jax.ShapeDtypeStruct((SHARE * NB * 2, CH...  51.2 us
    convert_element_type x1, other arithmetic, body(): return rows.reshape(SHARE, NB, 2, CH).transpose(0, 2, 1, 3).astype(BF16)  1.32 us
    unnamed x4, local copies, waits for them, and re-layouts  1.31 us

profile of v3, /device:TPU:1, one launch (start us, length us, event | category | flops | bytes accessed | tf_op | source)
XLA Modules:
  0.0 53.9 jit_solution(17922455835908972106)
XLA Ops:
  0.0 0.0 copy-start
  0.0 0.7 %copy-done = s32[2]{0:T(128)S(1)} copy-done((s32[2]{0:T(128)S(1)}, s32[2]{0:T(128)}, u32[]{:S(2)}) %copy-start) | copy-done | bytes 32
  0.7 0.0 copy-start.1
  0.7 0.7 %copy-done.1 = s32[2]{0:T(128)S(1)} copy-done((s32[2]{0:T(128)S(1)}, s32[2]{0:T(128)}, u32[]{:S(2)}) %copy-start.1) | copy-done | bytes 32
  1.3 51.2 %cross_spectra.1 = f32[6400,128]{1,0:T(8,128)S(1)} custom-call(s32[2]{0:T(128)S(1)} %copy-done, s32[2]{0:T(128)S(1)} %copy-done.1, bf16[32000,128]{1,0:T(8,128)(2,1)} %raw_ref.1), custom_call_target="tpu_custom_call" | custom-call | tf_op jit(solution)/shard_map/cross_spectra/pallas_call | solution.py:591
  52.5 1.3 %convert_element_type.9 = bf16[6400,128]{1,0:T(8,128)(2,1)} convert(f32[6400,128]{1,0:T(8,128)S(1)} %cross_spectra.1) | non-fusion elementwise | flops 819200 | bytes 4915200 | tf_op jit(solution)/shard_map/convert_element_type | solution.py:635
Async XLA Ops:
  0.0 0.7 %copy-start = (s32[2]{0:T(128)S(1)}, s32[2]{0:T(128)}, u32[]{:S(2)}) copy-start(s32[2]{0:T(128)} %blocks_hbm.1) | copy-start | bytes 28
  0.7 0.7 %copy-start.1 = (s32[2]{0:T(128)S(1)}, s32[2]{0:T(128)}, u32[]{:S(2)}) copy-start(s32[2]{0:T(128)} %band_hbm.1) | copy-start | bytes 28

commit v4 on v3

--- a/solution.py
+++ b/solution.py
@@ -103,10 +103,10 @@
 
 
 def kernel(
-    blocks_hbm, band_hbm, raw_ref, out_ref,
-    blocks_ref, band_ref, table_v, filter_v, within_v, raw_v, dec_v, en_v, run_v, norm_v, white_v, total_v, totals_v,
+    small_hbm, raw_ref, out_ref,
+    blocks_ref, table_v, filter_v, within_v, raw_v, dec_v, en_v, run_v, norm_v, white_v, total_v, totals_v,
     own_v, first_v, share_v, shares_v, rows_v, pieces_v, rising_v, weights_v,
-    small_sem, raw_sem, halo_sem, tot_sem, a_sem, b_sem, own_ssem, own_rsem, hand_sem, q_ssem, q_rsem,
+    small_sem, raw_sem, halo_sem, tot_ssem, tot_rsem, a_sem, b_sem, own_ssem, own_rsem, hand_sem, q_ssem, q_rsem,
 ):
     tm = lax.axis_index("tm")
     chan = lax.axis_index("chan")
@@ -129,18 +129,6 @@
     def line_device(other):
         return (other % 8, (other // 8) * 16 + pid)
 
-    barrier = pltpu.get_barrier_semaphore()
-
-    def greet(n):
-        pl.semaphore_signal(
-            barrier, inc=1, device_id=line_device((line + n + 1) % 16), device_id_type=MESH
-        )
-        pl.semaphore_signal(
-            barrier, inc=1, device_id=plane_device((pid + n + 1) % 16), device_id_type=MESH
-        )
-
-    repeat(15, greet)
-
     def chunk(c):
         first, last = CHUNKS[c], CHUNKS[c + 1]
         return pltpu.make_async_copy(
@@ -152,13 +140,25 @@
     small = [
         pltpu.make_async_copy(source, target, small_sem.at[n])
         for n, (source, target) in enumerate(
-            ((blocks_hbm, blocks_ref), (band_hbm, band_ref))
+            ((small_hbm, blocks_ref),)
         )
     ]
     for c in range(6):
         chunk(c).start()
     small[0].start()
-    small[1].start()
+
+    barrier = pltpu.get_barrier_semaphore()
+
+    def greet(n):
+        pl.semaphore_signal(
+            barrier, inc=1, device_id=line_device((line + n + 1) % 16), device_id_type=MESH
+        )
+        pl.semaphore_signal(
+            barrier, inc=1, device_id=plane_device((pid + n + 1) % 16), device_id_type=MESH
+        )
+
+    repeat(15, greet)
+
     raw_v[HALO + ROWS : RAW_PAD, :] = jnp.zeros((RAW_PAD - HALO - ROWS, CH), BF16)
     en_v[DEC_PAD:EN_PAD, :] = jnp.zeros((EN_PAD - DEC_PAD, CH), BF16)
     dec_v[DEC_PAD:EN_PAD, :] = jnp.zeros((EN_PAD - DEC_PAD, CH), F32)
@@ -241,17 +241,20 @@
     total = lax.fori_loop(0, 6, stretch, jnp.zeros((8, CH), F32))
     total_v[...] = jnp.broadcast_to(jnp.sum(total, axis=0, keepdims=True), (8, CH))
 
-    def total_to(other):
+    def total_to(other, group, slot):
         return pltpu.make_async_remote_copy(
             src_ref=total_v,
-            dst_ref=totals_v.at[tm],
-            send_sem=tot_sem.at[0],
-            recv_sem=tot_sem.at[1],
+            dst_ref=totals_v.at[group],
+            send_sem=tot_ssem.at[slot],
+            recv_sem=tot_rsem.at[group],
             device_id=(other, chan),
             device_id_type=MESH,
         )
 
-    repeat(7, lambda n: total_to((tm + n + 1) % 8).start())
+    def total_sent(n):
+        return total_to(tm + 1 + n, tm, n)
+
+    lax.fori_loop(0, 7 - tm, lambda n, carry: (total_sent(n).start(), carry)[1], 0)
 
     def arrived(ref, sem):
         pltpu.make_async_remote_copy(
@@ -272,8 +275,13 @@
         run_v[pl.ds(row, EB), :] = both[:, :CH]
         run_v[pl.ds(row + EB, EB), :] = both[:, CH:]
 
-    repeat(EN_PAD // (2 * EB), local_run)
-    arrived(totals_v.at[pl.ds(0, 7)], tot_sem.at[1])
+    repeat(EN_PAD // (4 * EB), lambda n: (local_run(2 * n), local_run(2 * n + 1)))
+
+    def total_taken(group, carry):
+        total_to((tm + 1) % 8, group, 0).wait_recv()
+        return carry
+
+    lax.fori_loop(0, tm, total_taken, 0)
 
     state = jnp.zeros((8, CH), F32)
     for group in range(7):
@@ -286,11 +294,12 @@
         norm_v[pl.ds(row, EB), :] = values.astype(BF16)
         return jnp.broadcast_to(running[EB - 1 : EB, :], (8, CH))
 
-    lax.fori_loop(0, OUTS // EB + 1, normalize, state)
+    lax.fori_loop(
+        0, EN_PAD // (2 * EB), lambda n, s: normalize(2 * n + 1, normalize(2 * n, s)), state
+    )
 
     small[0].wait()
-    small[1].wait()
-    low, high = band_ref[0], band_ref[1]
+    low, high = blocks_ref[2], blocks_ref[3]
     row_id = lax.broadcasted_iota(jnp.int32, (2 * NB, CH), 0)
     bin_id = jnp.where(row_id < 2 * MAIN, row_id % MAIN, MAIN + row_id % 4)
     keep = jnp.where((bin_id >= low) & (bin_id < high), 1.0, 0.0).astype(F32)
@@ -495,7 +504,10 @@
         for t in range(2):
             wait_half(h, 3 - 2 * t, 0, h * 11 + t)
             forward(h, 3 - 2 * t, 0, True, t, h * 11 + 2)
-            send_across(h, 3 - 2 * t)
+
+    def near_spread(h):
+        send_across(h, 3)
+        send_across(h, 1)
 
     def near_across(h, f):
         for t in range(2):
@@ -509,12 +521,11 @@
     repeat(2, own_half)
     repeat(2, lambda h: send_across(h, 0))
     repeat(2, near_along)
+    repeat(2, near_spread)
+    relay_own(2)
     repeat(2, lambda h: near_across(h, 0))
     repeat(2, far_along)
-    relay_own(2)
-    repeat(6, lambda n: near_across(n % 2, n // 2 + 1))
     relay_own(3)
-    arrived(own_v.at[pl.ds(0, 4)], hand_sem.at[1])
 
     scale = 1.0 / math.sqrt(8 * NW)
 
@@ -533,18 +544,6 @@
             im.append(-rows[0:16])
         rhs = jnp.concatenate([jnp.concatenate(re, axis=0), jnp.concatenate(im, axis=0)], axis=1)
         put(k, lhs, rhs)
-
-    def near_bin(n):
-        f, s = n % 3, n // 3
-        main_bin(at(0, f + f // 2, s + s // 2))
-
-    def far_bin(n):
-        late, m = n // 4, n % 4
-        main_bin(at(0, 2 * (1 - late) + late * (m + m // 2), m * (1 - late) + 2 * late))
-
-    repeat(9, near_bin)
-    arrived(pieces_v.at[pl.ds(0, 4)], q_rsem.at[22])
-    repeat(7, far_bin)
 
     sign = jnp.where(lax.broadcasted_iota(jnp.int32, (8, CH), 0) < 4, 1.0, -1.0).astype(F32)
 
@@ -566,13 +565,28 @@
         rhs = jnp.concatenate([jnp.concatenate(re, axis=0), jnp.concatenate(im, axis=0)], axis=1)
         put(MAIN + kk, lhs, rhs.astype(BF16))
 
-    repeat(NB - MAIN, tail_bin)
+    repeat(2, lambda h: near_across(h, 1))
+    arrived(own_v.at[pl.ds(0, 4)], hand_sem.at[1])
+    main_bin(pid)
+    main_bin(at(0, 1, 0))
+    repeat(2, lambda h: near_across(h, 2))
+    main_bin(at(0, 3, 0))
+    main_bin(at(0, 0, 1))
+    repeat(2, lambda h: near_across(h, 3))
+    main_bin(at(0, 0, 3))
+    for f in (1, 3):
+        for s in (1, 3):
+            main_bin(at(0, f, s))
+    arrived(pieces_v.at[pl.ds(0, 4)], q_rsem.at[22])
+    for f, s in ((2, 0), (2, 1), (2, 2), (2, 3), (0, 2), (1, 2), (3, 2)):
+        main_bin(at(0, f, s))
+    unrolled(NB - MAIN, tail_bin)
 
     @pl.when(tm < 7)
     def _():
         halo_to(tm + 1).wait_send()
 
-    departed(totals_v.at[pl.ds(0, 7)], tot_sem.at[0])
+    lax.fori_loop(0, 7 - tm, lambda n, carry: (total_sent(n).wait_send(), carry)[1], 0)
     departed(first_v.at[pl.ds(0, 15)], a_sem.at[0])
     departed(shares_v.at[pl.ds(0, 15)], b_sem.at[0])
     departed(own_v.at[pl.ds(0, 4)], hand_sem.at[0])
@@ -591,11 +605,10 @@
     rows = pl.pallas_call(
         kernel,
         out_shape=jax.ShapeDtypeStruct((SHARE * NB * 2, CH), F32),
-        in_specs=[hbm] * 3,
+        in_specs=[hbm] * 2,
         out_specs=vmem,
         scratch_shapes=[
-            pltpu.SMEM((2,), jnp.int32),
-            pltpu.SMEM((2,), jnp.int32),
+            pltpu.SMEM((4,), jnp.int32),
             pltpu.VMEM((4, DR, 512), BF16),
             pltpu.VMEM((MB, KB), BF16),
             pltpu.VMEM((EB, EB), BF16),
@@ -618,7 +631,8 @@
             dma((2,)),
             dma((6,)),
             dma((2,)),
-            dma((2,)),
+            dma((7,)),
+            dma((7,)),
             dma((2,)),
             dma((2,)),
             dma((6,)),
@@ -631,7 +645,7 @@
             collective_id=0, has_side_effects=True, vmem_limit_bytes=50 * 2**20
         ),
         name="cross_spectra",
-    )(source_blocks, band_bins, raw_strain)
+    )(jnp.concatenate([source_blocks, band_bins]), raw_strain)
     return rows.reshape(SHARE, NB, 2, CH).transpose(0, 2, 1, 3).astype(BF16)
 
 

time: 54 us -> 48 us (0.89)
  Pallas kernels: 51.2 us -> 45.9 us
  local copies, waits for them, and re-layouts: 1.31 us -> 0 us
  other arithmetic: 1.32 us -> 2.07 us
    pallas_call x1, Pallas kernels: 51.2 us -> 45.9 us  [body(): pl.pallas_call(kernel, out_shape=jax.ShapeDtypeStruct((SHARE * NB * 2, CH...]
    unnamed x4 -> x0, local copies, waits for them, and re-layouts: 1.31 us -> none
    concatenate x0 -> x1, other arithmetic: none -> 0.75 us  [body(): jnp.concatenate([source_blocks, band_bins])]
where the time goes in v4:
time: 48 us
  Pallas kernels  45.9 us (96%)
  other arithmetic  2.07 us (4%)
    pallas_call x1, Pallas kernels, body(): pl.pallas_call(kernel, out_shape=jax.ShapeDtypeStruct((SHARE * NB * 2, CH...  45.9 us
    convert_element_type x1, other arithmetic, body(): return rows.reshape(SHARE, NB, 2, CH).transpose(0, 2, 1, 3).astype(BF16)  1.32 us

profile of v4, /device:TPU:1, one launch (start us, length us, event | category | flops | bytes accessed | tf_op | source)
XLA Modules:
  0.0 48.0 jit_solution(13971008262253717827)
XLA Ops:
  0.0 0.7 %pad_add_fusion.small_hbm = s32[4]{0:T(128)S(1)} fusion(s32[2]{0:T(128)} %param.5, s32[2]{0:T(128)} %param.4), kind=kLoop, calls=%fused_computation | loop fusion | flops 4 | bytes 32 | tf_op jit(solution)/shard_map/concatenate | solution.py:648
  0.7 45.9 %cross_spectra.1 = f32[6400,128]{1,0:T(8,128)S(1)} custom-call(s32[4]{0:T(128)S(1)} %pad_add_fusion.small_hbm, bf16[32000,128]{1,0:T(8,128)(2,1)} %raw_ref.1), custom_call_target="tpu_custom_call" | custom-call | tf_op jit(solution)/shard_map/cross_spectra/pallas_call | solution.py:605
  46.6 1.3 %convert_element_type.9 = bf16[6400,128]{1,0:T(8,128)(2,1)} convert(f32[6400,128]{1,0:T(8,128)S(1)} %cross_spectra.1) | non-fusion elementwise | flops 819200 | bytes 4915200 | tf_op jit(solution)/shard_map/convert_element_type | solution.py:649

commit v5 on v4

--- a/solution.py
+++ b/solution.py
@@ -54,7 +54,7 @@
     return values / values.sum()
 
 
-def make_tables(table_v, filter_v, within_v):
+def make_filter(filter_v):
     taps = lowpass_taps().astype(jnp.bfloat16).astype(np.float32)
     row = lax.broadcasted_iota(jnp.int32, (8, CH), 0)
     lane = lax.broadcasted_iota(jnp.int32, (8, CH), 1)
@@ -77,6 +77,11 @@
                     columns.append(jnp.zeros((8, CH), F32))
             rows.append(jnp.concatenate(columns, axis=1))
         filter_v[16 * b : 16 * b + 16, :] = jnp.concatenate(rows, axis=0).astype(BF16)
+
+
+def make_tables(table_v, within_v, rising_v):
+    place = lax.broadcasted_iota(jnp.int32, (EB, CH), 0).astype(F32)
+    rising_v[...] = jnp.exp((place + 1.0) * (-1.0 / WIN))
     gap = lax.broadcasted_iota(jnp.int32, (EB, EB), 0) - lax.broadcasted_iota(jnp.int32, (EB, EB), 1)
     share = (1.0 - FORGET) * jnp.exp(jnp.maximum(gap, 0).astype(F32) * (-1.0 / WIN))
     within_v[...] = jnp.where(gap >= 0, share, 0.0).astype(BF16)
@@ -105,7 +110,7 @@
 def kernel(
     small_hbm, raw_ref, out_ref,
     blocks_ref, table_v, filter_v, within_v, raw_v, dec_v, en_v, run_v, norm_v, white_v, total_v, totals_v,
-    own_v, first_v, share_v, shares_v, rows_v, pieces_v, rising_v, weights_v,
+    own_v, first_v, share_v, shares_v, rows_v, pieces_v, rising_v, weights_v, eye_v,
     small_sem, raw_sem, halo_sem, tot_ssem, tot_rsem, a_sem, b_sem, own_ssem, own_rsem, hand_sem, q_ssem, q_rsem,
 ):
     tm = lax.axis_index("tm")
@@ -184,9 +189,7 @@
     weights_v[1] = jnp.where(
         back <= 0.0, (1.0 - FORGET) * jnp.exp(jnp.minimum(back, 0.0) * (1.0 / WIN)), 0.0
     )
-    place = lax.broadcasted_iota(jnp.int32, (EB, CH), 0).astype(F32)
-    rising_v[...] = jnp.exp((place + 1.0) * (-1.0 / WIN))
-    make_tables(table_v, filter_v, within_v)
+    make_filter(filter_v)
 
     block_fade = FORGET**MB
     tail_fade = FORGET**tail
@@ -255,6 +258,7 @@
         return total_to(tm + 1 + n, tm, n)
 
     lax.fori_loop(0, 7 - tm, lambda n, carry: (total_sent(n).start(), carry)[1], 0)
+    make_tables(table_v, within_v, rising_v)
 
     def arrived(ref, sem):
         pltpu.make_async_remote_copy(
@@ -396,6 +400,11 @@
         def _():
             hand_over(above).start()
 
+    eye = (
+        lax.broadcasted_iota(jnp.int32, (SHARE, 256), 0)
+        == lax.broadcasted_iota(jnp.int32, (SHARE, 256), 1)
+    )
+    eye_v[...] = jnp.where(eye, 1.0, 0.0).astype(BF16)
     first_v[pid] = own_v[tm, pid]
     arrived(first_v.at[pl.ds(0, 15)], a_sem.at[1])
 
@@ -453,13 +462,8 @@
         rows_v[pl.ds(pl.multiple_of(320 + g * 8, 8), 8), :] = rows[32:40]
 
     unrolled(8, unpack)
-    eye = (
-        lax.broadcasted_iota(jnp.int32, (SHARE, 256), 0)
-        == lax.broadcasted_iota(jnp.int32, (SHARE, 256), 1)
-    )
-    eye = jnp.where(eye, 1.0, 0.0).astype(BF16)
     turned = lax.dot_general(
-        eye, rows_v[...].astype(BF16), (((1,), (1,)), ((), ())), preferred_element_type=F32
+        eye_v[...], rows_v[...].astype(BF16), (((1,), (1,)), ((), ())), preferred_element_type=F32
     )
     half_lane = lax.broadcasted_iota(jnp.int32, (80, CH), 1) < 64
     packed_tail = jnp.where(half_lane, turned[0:80, 2 * CH :], turned[80:160, 2 * CH :])
@@ -496,18 +500,25 @@
             h, f, s, step if along else 0, 0 if along else step, first, count, event
         ).start()
 
+    def along_rows(t, late):
+        return ((0, FR), (FR, HR - FR))[t if late == 0 else 1 - t]
+
     def own_half(h):
-        for t in range(2):
-            piece_copy(h, 0, 0, 1 + 2 * t, 0, 0, HR, h * 11 + t).start()
+        for late in range(2):
+            for t in range(2):
+                event = h * 11 + t if late == 0 else 23 + 2 * h + t
+                first, count = along_rows(t, late)
+                piece_copy(h, 0, 0, 1 + 2 * t, 0, first, count, event).start()
 
     def near_along(h):
         for t in range(2):
-            wait_half(h, 3 - 2 * t, 0, h * 11 + t)
+            piece_copy(h, 3 - 2 * t, 0, 1, 0, *along_rows(t, 0), h * 11 + t).wait_recv()
             forward(h, 3 - 2 * t, 0, True, t, h * 11 + 2)
 
     def near_spread(h):
-        send_across(h, 3)
-        send_across(h, 1)
+        for t in range(2):
+            piece_copy(h, 3 - 2 * t, 0, 1, 0, *along_rows(t, 1), 23 + 2 * h + t).wait_recv()
+            send_across(h, 3 - 2 * t)
 
     def near_across(h, f):
         for t in range(2):
@@ -520,9 +531,9 @@
 
     repeat(2, own_half)
     repeat(2, lambda h: send_across(h, 0))
+    relay_own(2)
     repeat(2, near_along)
     repeat(2, near_spread)
-    relay_own(2)
     repeat(2, lambda h: near_across(h, 0))
     repeat(2, far_along)
     relay_own(3)
@@ -569,10 +580,10 @@
     arrived(own_v.at[pl.ds(0, 4)], hand_sem.at[1])
     main_bin(pid)
     main_bin(at(0, 1, 0))
-    repeat(2, lambda h: near_across(h, 2))
+    repeat(2, lambda h: near_across(h, 3))
     main_bin(at(0, 3, 0))
     main_bin(at(0, 0, 1))
-    repeat(2, lambda h: near_across(h, 3))
+    repeat(2, lambda h: near_across(h, 2))
     main_bin(at(0, 0, 3))
     for f in (1, 3):
         for s in (1, 3):
@@ -628,6 +639,7 @@
             pltpu.VMEM((16, QR, CH), BF16),
             pltpu.VMEM((EB, CH), F32),
             pltpu.VMEM((2, MB, CH), F32),
+            pltpu.VMEM((SHARE, 256), BF16),
             dma((2,)),
             dma((6,)),
             dma((2,)),
@@ -639,7 +651,7 @@
             dma((4,)),
             dma((2,)),
             dma((1,)),
-            dma((23,)),
+            dma((27,)),
         ],
         compiler_params=pltpu.CompilerParams(
             collective_id=0, has_side_effects=True, vmem_limit_bytes=50 * 2**20

time: 48 us -> 46.8 us (0.975); the launches traced: 48 us -> 46.2 us
  Pallas kernels: 45.9 us -> 44.1 us
    pallas_call x1, Pallas kernels: 45.9 us -> 44.1 us  [body(): pl.pallas_call(kernel, out_shape=jax.ShapeDtypeStruct((SHARE * NB * 2, CH...]
where the time goes in v5:
time: 46.8 us; the launch traced here: 46.2 us
  Pallas kernels  44.1 us (94%)
  other arithmetic  2.07 us (4%)
    pallas_call x1, Pallas kernels, body(): pl.pallas_call(kernel, out_shape=jax.ShapeDtypeStruct((SHARE * NB * 2, CH...  44.1 us
    convert_element_type x1, other arithmetic, body(): return rows.reshape(SHARE, NB, 2, CH).transpose(0, 2, 1, 3).astype(BF16)  1.32 us

profile of v5, /device:TPU:1, one launch (start us, length us, event | category | flops | bytes accessed | tf_op | source)
XLA Modules:
  0.0 46.2 jit_solution(1466267837896745988)
XLA Ops:
  0.0 0.7 %pad_add_fusion.small_hbm = s32[4]{0:T(128)S(1)} fusion(s32[2]{0:T(128)} %param.5, s32[2]{0:T(128)} %param.4), kind=kLoop, calls=%fused_computation | loop fusion | flops 4 | bytes 32 | tf_op jit(solution)/shard_map/concatenate | solution.py:660
  0.7 44.1 %cross_spectra.1 = f32[6400,128]{1,0:T(8,128)S(1)} custom-call(s32[4]{0:T(128)S(1)} %pad_add_fusion.small_hbm, bf16[32000,128]{1,0:T(8,128)(2,1)} %raw_ref.1), custom_call_target="tpu_custom_call" | custom-call | tf_op jit(solution)/shard_map/cross_spectra/pallas_call | solution.py:616
  44.9 1.3 %convert_element_type.9 = bf16[6400,128]{1,0:T(8,128)(2,1)} convert(f32[6400,128]{1,0:T(8,128)S(1)} %cross_spectra.1) | non-fusion elementwise | flops 819200 | bytes 4915200 | tf_op jit(solution)/shard_map/convert_element_type | solution.py:661

commit v6 on v5

--- a/solution.py
+++ b/solution.py
@@ -489,9 +489,14 @@
     def wait_half(h, f, s, event):
         piece_copy(h, f, s, 1, 0, 0, HR, event).wait_recv()
 
+    def rows_of(t, late):
+        return ((0, FR), (FR, HR - FR))[t if late == 0 else 1 - t]
+
     def send_across(h, f):
-        for t in range(2):
-            piece_copy(h, f, 0, 0, 1 + 2 * t, 0, HR, h * 11 + 3 + 2 * f + t).start()
+        for late in range(2):
+            for t in range(2):
+                event = h * 11 + 3 + 2 * f + t if late == 0 else 27 + f
+                piece_copy(h, f, 0, 0, 1 + 2 * t, *rows_of(t, late), event).start()
 
     def forward(h, f, s, along, t, event):
         first, count = ((0, FR), (FR, HR - FR))[t]
@@ -500,30 +505,30 @@
             h, f, s, step if along else 0, 0 if along else step, first, count, event
         ).start()
 
-    def along_rows(t, late):
-        return ((0, FR), (FR, HR - FR))[t if late == 0 else 1 - t]
-
     def own_half(h):
         for late in range(2):
             for t in range(2):
                 event = h * 11 + t if late == 0 else 23 + 2 * h + t
-                first, count = along_rows(t, late)
+                first, count = rows_of(t, late)
                 piece_copy(h, 0, 0, 1 + 2 * t, 0, first, count, event).start()
 
     def near_along(h):
         for t in range(2):
-            piece_copy(h, 3 - 2 * t, 0, 1, 0, *along_rows(t, 0), h * 11 + t).wait_recv()
+            piece_copy(h, 3 - 2 * t, 0, 1, 0, *rows_of(t, 0), h * 11 + t).wait_recv()
             forward(h, 3 - 2 * t, 0, True, t, h * 11 + 2)
 
     def near_spread(h):
         for t in range(2):
-            piece_copy(h, 3 - 2 * t, 0, 1, 0, *along_rows(t, 1), 23 + 2 * h + t).wait_recv()
+            piece_copy(h, 3 - 2 * t, 0, 1, 0, *rows_of(t, 1), 23 + 2 * h + t).wait_recv()
             send_across(h, 3 - 2 * t)
 
     def near_across(h, f):
         for t in range(2):
-            wait_half(h, f, 3 - 2 * t, h * 11 + 3 + 2 * f + t)
+            piece_copy(h, f, 3 - 2 * t, 1, 0, *rows_of(t, 0), h * 11 + 3 + 2 * f + t).wait_recv()
             forward(h, f, 3 - 2 * t, False, t, 22)
+
+    def late_across(f):
+        arrived(pieces_v.at[pl.ds(0, 1)], q_rsem.at[27 + f])
 
     def far_along(h):
         wait_half(h, 2, 0, h * 11 + 2)
@@ -533,8 +538,8 @@
     repeat(2, lambda h: send_across(h, 0))
     relay_own(2)
     repeat(2, near_along)
+    repeat(2, lambda h: near_across(h, 0))
     repeat(2, near_spread)
-    repeat(2, lambda h: near_across(h, 0))
     repeat(2, far_along)
     relay_own(3)
 
@@ -578,6 +583,7 @@
 
     repeat(2, lambda h: near_across(h, 1))
     arrived(own_v.at[pl.ds(0, 4)], hand_sem.at[1])
+    late_across(0)
     main_bin(pid)
     main_bin(at(0, 1, 0))
     repeat(2, lambda h: near_across(h, 3))
@@ -585,9 +591,12 @@
     main_bin(at(0, 0, 1))
     repeat(2, lambda h: near_across(h, 2))
     main_bin(at(0, 0, 3))
+    late_across(1)
+    late_across(3)
     for f in (1, 3):
         for s in (1, 3):
             main_bin(at(0, f, s))
+    late_across(2)
     arrived(pieces_v.at[pl.ds(0, 4)], q_rsem.at[22])
     for f, s in ((2, 0), (2, 1), (2, 2), (2, 3), (0, 2), (1, 2), (3, 2)):
         main_bin(at(0, f, s))
@@ -651,7 +660,7 @@
             dma((4,)),
             dma((2,)),
             dma((1,)),
-            dma((27,)),
+            dma((31,)),
         ],
         compiler_params=pltpu.CompilerParams(
             collective_id=0, has_side_effects=True, vmem_limit_bytes=50 * 2**20

time: 46.8 us -> 46.6 us (level); the launches traced: 46.2 us -> 46.5 us
  no operation moved by 1% of the time
where the time goes in v6:
time: 46.6 us; the launch traced here: 46.5 us
  Pallas kernels  44.5 us (95%)
  other arithmetic  2.07 us (4%)
    pallas_call x1, Pallas kernels, body(): pl.pallas_call(kernel, out_shape=jax.ShapeDtypeStruct((SHARE * NB * 2, CH...  44.5 us
    convert_element_type x1, other arithmetic, body(): return rows.reshape(SHARE, NB, 2, CH).transpose(0, 2, 1, 3).astype(BF16)  1.32 us

profile of v6, /device:TPU:1, one launch (start us, length us, event | category | flops | bytes accessed | tf_op | source)
XLA Modules:
  0.0 46.5 jit_solution(4670392845852497773)
XLA Ops:
  0.0 0.7 %pad_add_fusion.small_hbm = s32[4]{0:T(128)S(1)} fusion(s32[2]{0:T(128)} %param.5, s32[2]{0:T(128)} %param.4), kind=kLoop, calls=%fused_computation | loop fusion | flops 4 | bytes 32 | tf_op jit(solution)/shard_map/concatenate | solution.py:669
  0.7 44.5 %cross_spectra.1 = f32[6400,128]{1,0:T(8,128)S(1)} custom-call(s32[4]{0:T(128)S(1)} %pad_add_fusion.small_hbm, bf16[32000,128]{1,0:T(8,128)(2,1)} %raw_ref.1), custom_call_target="tpu_custom_call" | custom-call | tf_op jit(solution)/shard_map/cross_spectra/pallas_call | solution.py:625
  45.2 1.3 %convert_element_type.9 = bf16[6400,128]{1,0:T(8,128)(2,1)} convert(f32[6400,128]{1,0:T(8,128)S(1)} %cross_spectra.1) | non-fusion elementwise | flops 819200 | bytes 4915200 | tf_op jit(solution)/shard_map/convert_element_type | solution.py:670

commit v7 on v5

--- a/solution.py
+++ b/solution.py
@@ -533,8 +533,8 @@
     repeat(2, lambda h: send_across(h, 0))
     relay_own(2)
     repeat(2, near_along)
+    repeat(2, lambda h: near_across(h, 0))
     repeat(2, near_spread)
-    repeat(2, lambda h: near_across(h, 0))
     repeat(2, far_along)
     relay_own(3)
 

time: 46.8 us -> 47.2 us (level); the launches traced: 46.2 us -> 47.1 us
  Pallas kernels: 44.1 us -> 45 us
    pallas_call x1, Pallas kernels: 44.1 us -> 45 us  [body(): pl.pallas_call(kernel, out_shape=jax.ShapeDtypeStruct((SHARE * NB * 2, CH...]
where the time goes in v7:
time: 47.2 us; the launch traced here: 47.1 us
  Pallas kernels  45 us (95%)
  other arithmetic  2.07 us (4%)
    pallas_call x1, Pallas kernels, body(): pl.pallas_call(kernel, out_shape=jax.ShapeDtypeStruct((SHARE * NB * 2, CH...  45 us
    convert_element_type x1, other arithmetic, body(): return rows.reshape(SHARE, NB, 2, CH).transpose(0, 2, 1, 3).astype(BF16)  1.32 us

profile of v7, /device:TPU:1, one launch (start us, length us, event | category | flops | bytes accessed | tf_op | source)
XLA Modules:
  0.0 47.1 jit_solution(1541184534642321858)
XLA Ops:
  0.0 0.7 %pad_add_fusion.small_hbm = s32[4]{0:T(128)S(1)} fusion(s32[2]{0:T(128)} %param.5, s32[2]{0:T(128)} %param.4), kind=kLoop, calls=%fused_computation | loop fusion | flops 4 | bytes 32 | tf_op jit(solution)/shard_map/concatenate | solution.py:660
  0.7 45.0 %cross_spectra.1 = f32[6400,128]{1,0:T(8,128)S(1)} custom-call(s32[4]{0:T(128)S(1)} %pad_add_fusion.small_hbm, bf16[32000,128]{1,0:T(8,128)(2,1)} %raw_ref.1), custom_call_target="tpu_custom_call" | custom-call | tf_op jit(solution)/shard_map/cross_spectra/pallas_call | solution.py:616
  45.8 1.3 %convert_element_type.9 = bf16[6400,128]{1,0:T(8,128)(2,1)} convert(f32[6400,128]{1,0:T(8,128)S(1)} %cross_spectra.1) | non-fusion elementwise | flops 819200 | bytes 4915200 | tf_op jit(solution)/shard_map/convert_element_type | solution.py:661
